TPU v7x, 32 devices: a whole 2x2x4 slice. The times are simulated.
32 devices in a mesh: dp: 8 (over z, y), tensor: 4 (over x, core).
Axes of the slice: x: 2, y: 2, z: 4, core: 2. Of those that a mesh axis runs over, the one named last changes fastest.
Arguments:
- tokens: bfloat16 [12288, 1280], P('dp'), may hold values from -6 to 6
- clip_len: int32 [5], replicated, may hold values from 31 to 1500, as said below
- slot_clip: int32 [8], P('dp'), may hold values from -1 to 4, as said below
- w_qkv: bfloat16 [1280, 3, 1280], P(None, None, 'tensor'), may hold values from -0.15625 to 0.15625
- bias_q: float32 [1280], P('tensor'), may hold values from -1.5 to 1.5
- bias_v: float32 [1280], P('tensor'), may hold values from -1.5 to 1.5
- w_out: bfloat16 [1280, 1280], P('tensor'), may hold values from -0.625 to 0.625
- bias_out: float32 [1280], replicated, may hold values from -1.5 to 1.5
- w_up: bfloat16 [1280, 5120], P(None, 'tensor'), may hold values from -0.15625 to 0.15625
- bias_up: float32 [5120], P('tensor'), may hold values from -1.5 to 1.5
- w_down: bfloat16 [5120, 1280], P('tensor'), may hold values from -0.078125 to 0.078125
- bias_down: float32 [1280], replicated, may hold values from -1.5 to 1.5
- gain1: float32 [1280], replicated, may hold values from 0.1 to 1.9
- shift1: float32 [1280], replicated, may hold values from -1.5 to 1.5
- gain2: float32 [1280], replicated, may hold values from 0.1 to 1.9
- shift2: float32 [1280], replicated, may hold values from -1.5 to 1.5
- grad_out: bfloat16 [12288, 1280], P('dp')
Outputs:
- mixed: bfloat16 [12288, 1280], P('dp')
- grad_tokens: float32 [12288, 1280], P('dp')
- grad_qkv: float32 [1280, 3, 1280], P(None, None, 'tensor')
- grad_bias_q: float32 [1280], P('tensor')
- grad_bias_v: float32 [1280], P('tensor')
- grad_out_proj: float32 [1280, 1280], P('tensor')
- grad_out_bias: float32 [1280], replicated
- grad_up: float32 [1280, 5120], P(None, 'tensor')
- grad_up_bias: float32 [5120], P('tensor')
- grad_down: float32 [5120, 1280], P('tensor')
- grad_down_bias: float32 [1280], replicated
- grad_gain1: float32 [1280], replicated
- grad_shift1: float32 [1280], replicated
- grad_gain2: float32 [1280], replicated
- grad_shift2: float32 [1280], replicated
Inputs may be any that keep to these rules, and one draw needn't show every extreme that they name: `clip_len`: some clip has exactly 1500 frames in every draw; short clips are far more common than long ones. `slot_clip`: every clip stands in exactly one slot; the other slots hold -1; each index of dp holds one slot; some slots are empty (-1), and the clip lengths in the filled slots vary widely.
All inputs are finite; a program needn't handle non-finite values.
Results may differ from a plain program's by a relative error of at most 0.022.
Values may be sent and summed in bfloat16 or wider, within the bound.
A program may use at most 256 MiB of HBM per device.

v0:
```python
import jax
import jax.numpy as jnp
from jax import lax
from jax.sharding import PartitionSpec as P

HD = 64


EPS = 1e-05
NEG = -1e30
HALF_ROOT = 0.7071067811865476
INV_ROOT_TAU = 0.3989422804014327


def layer_norm(value, gain, shift):
    center = value - jnp.mean(value, -1, keepdims=True)
    rstd = lax.rsqrt(jnp.mean(center * center, -1, keepdims=True) + EPS)
    normed = center * rstd
    return (normed, rstd, normed * gain + shift)


def layer_norm_back(grad, normed, rstd, gain):
    scaled = grad * gain
    return rstd * (
        scaled
        - jnp.mean(scaled, -1, keepdims=True)
        - normed * jnp.mean(scaled * normed, -1, keepdims=True)
    )


def gelu_pair(value):
    cdf = 0.5 * (1.0 + jax.scipy.special.erf(value * HALF_ROOT))
    return (value * cdf, cdf + value * jnp.exp(-0.5 * value * value) * INV_ROOT_TAU)


def contract_first(left, right):
    return lax.dot_general(
        left, right, (((0,), (0,)), ((), ())), preferred_element_type=jnp.float32
    )


def contract_last(left, right):
    return lax.dot_general(
        left, right, (((1,), (1,)), ((), ())), preferred_element_type=jnp.float32
    )


def masked_scores(query_clip, keys_clip, length, positions, scale):
    raw = (
        jnp.einsum("qhe,khe->hqk", query_clip, keys_clip, preferred_element_type=jnp.float32)
        * scale
    )
    return jnp.where((positions < length)[None, None, :], raw, NEG)


def shards(
    tokens,
    clip_len,
    slot_clip,
    w_qkv,
    bias_q,
    bias_v,
    w_out,
    bias_out,
    w_up,
    bias_up,
    w_down,
    bias_down,
    gain1,
    shift1,
    gain2,
    shift2,
    grad_out,
):
    rows, width = tokens.shape
    clips = slot_clip.shape[0]
    cap = rows // clips
    local = w_qkv.shape[2]
    heads = local // HD
    scale = HD ** (-0.5)
    positions = jnp.arange(cap, dtype=jnp.int32)
    match = slot_clip[:, None] == jnp.arange(clip_len.shape[0], dtype=jnp.int32)[None, :]
    lengths = jnp.sum(jnp.where(match, clip_len[None, :], 0), 1)
    valid = (positions[None, :] < lengths[:, None]).reshape(rows, 1)
    source = tokens.astype(jnp.float32)
    normed1, rstd1, pre1 = layer_norm(source, gain1, shift1)
    act1 = pre1.astype(jnp.bfloat16)
    joined = w_qkv.reshape(width, 3 * local)
    proj = jnp.dot(act1, joined, preferred_element_type=jnp.float32)
    query = (proj[:, :local] + bias_q).astype(jnp.bfloat16)
    keys = proj[:, local : 2 * local].astype(jnp.bfloat16)
    values = (proj[:, 2 * local :] + bias_v).astype(jnp.bfloat16)

    def per_clip(value):
        return value.reshape(clips, cap, heads, HD)

    def forward_clip(inputs):
        query_clip, keys_clip, values_clip, length = inputs
        raw = masked_scores(query_clip, keys_clip, length, positions, scale)
        top = jnp.max(raw, -1, keepdims=True)
        lse = top + jnp.log(jnp.sum(jnp.exp(raw - top), -1, keepdims=True))
        probs = jnp.exp(raw - lse).astype(jnp.bfloat16)
        context_clip = jnp.einsum(
            "hqk,khe->qhe", probs, values_clip, preferred_element_type=jnp.float32
        )
        return (context_clip.astype(jnp.bfloat16), lse)

    context_all, lse_all = lax.map(
        forward_clip, (per_clip(query), per_clip(keys), per_clip(values), lengths)
    )
    context = context_all.reshape(rows, local)
    attended = lax.psum(
        jnp.dot(context, w_out, preferred_element_type=jnp.float32).astype(jnp.bfloat16), "tensor"
    ).astype(jnp.float32)
    middle = source + attended + bias_out
    normed2, rstd2, pre2 = layer_norm(middle, gain2, shift2)
    act2 = pre2.astype(jnp.bfloat16)
    pre = jnp.dot(act2, w_up, preferred_element_type=jnp.float32) + bias_up
    hidden_f, slope = gelu_pair(pre)
    hidden = hidden_f.astype(jnp.bfloat16)
    branch = lax.psum(
        jnp.dot(hidden, w_down, preferred_element_type=jnp.float32).astype(jnp.bfloat16), "tensor"
    ).astype(jnp.float32)
    mixed = jnp.where(valid, middle + branch + bias_down, 0.0).astype(jnp.bfloat16)
    upstream = jnp.where(valid, grad_out.astype(jnp.float32), 0.0)
    upstream_b = upstream.astype(jnp.bfloat16)
    g_down_bias = jnp.sum(upstream, 0)
    g_down = contract_first(hidden, upstream_b)
    d_pre = contract_last(upstream_b, w_down) * slope
    g_up_bias = jnp.sum(d_pre, 0)
    d_pre_b = d_pre.astype(jnp.bfloat16)
    g_up = contract_first(act2, d_pre_b)
    d_act2 = lax.psum(contract_last(d_pre_b, w_up).astype(jnp.bfloat16), "tensor").astype(
        jnp.float32
    )
    g_gain2 = jnp.sum(d_act2 * normed2, 0)
    g_shift2 = jnp.sum(d_act2, 0)
    d_middle = upstream + layer_norm_back(d_act2, normed2, rstd2, gain2)
    g_out_bias = jnp.sum(d_middle, 0)
    d_middle_b = d_middle.astype(jnp.bfloat16)
    g_out = contract_first(context, d_middle_b)
    d_context = contract_last(d_middle_b, w_out).astype(jnp.bfloat16)

    def backward_clip(inputs):
        query_clip, keys_clip, values_clip, context_clip, dcontext_clip, lse, length = inputs
        raw = masked_scores(query_clip, keys_clip, length, positions, scale)
        probs_f = jnp.exp(raw - lse)
        probs = probs_f.astype(jnp.bfloat16)
        d_probs = jnp.einsum(
            "qhe,khe->hqk", dcontext_clip, values_clip, preferred_element_type=jnp.float32
        )
        delta = jnp.sum(dcontext_clip.astype(jnp.float32) * context_clip.astype(jnp.float32), -1).T[
            :, :, None
        ]
        d_scores = (probs_f * (d_probs - delta) * scale).astype(jnp.bfloat16)
        d_query_clip = jnp.einsum(
            "hqk,khe->qhe", d_scores, keys_clip, preferred_element_type=jnp.float32
        )
        d_keys_clip = jnp.einsum(
            "hqk,qhe->khe", d_scores, query_clip, preferred_element_type=jnp.float32
        )
        d_values_clip = jnp.einsum(
            "hqk,qhe->khe", probs, dcontext_clip, preferred_element_type=jnp.float32
        )
        return (d_query_clip, d_keys_clip, d_values_clip)

    d_query, d_keys, d_values = lax.map(
        backward_clip,
        (
            per_clip(query),
            per_clip(keys),
            per_clip(values),
            context_all,
            per_clip(d_context),
            lse_all,
            lengths,
        ),
    )
    d_query = d_query.reshape(rows, local)
    d_keys = d_keys.reshape(rows, local)
    d_values = d_values.reshape(rows, local)
    g_bias_q = jnp.sum(d_query, 0)
    g_bias_v = jnp.sum(d_values, 0)
    stacked = jnp.concatenate(
        [d_query.astype(jnp.bfloat16), d_keys.astype(jnp.bfloat16), d_values.astype(jnp.bfloat16)],
        1,
    )
    g_qkv = contract_first(act1, stacked).reshape(width, 3, local)
    d_act1 = lax.psum(contract_last(stacked, joined).astype(jnp.bfloat16), "tensor").astype(
        jnp.float32
    )
    g_gain1 = jnp.sum(d_act1 * normed1, 0)
    g_shift1 = jnp.sum(d_act1, 0)
    d_tokens = jnp.where(valid, d_middle + layer_norm_back(d_act1, normed1, rstd1, gain1), 0.0)
    (
        g_qkv,
        g_bias_q,
        g_bias_v,
        g_out,
        g_out_bias,
        g_up,
        g_up_bias,
        g_down,
        g_down_bias,
        g_gain1,
        g_shift1,
        g_gain2,
        g_shift2,
    ) = (
        lax.psum(g_qkv.astype(jnp.bfloat16), "dp").astype(jnp.float32),
        lax.psum(g_bias_q.astype(jnp.bfloat16), "dp").astype(jnp.float32),
        lax.psum(g_bias_v.astype(jnp.bfloat16), "dp").astype(jnp.float32),
        lax.psum(g_out.astype(jnp.bfloat16), "dp").astype(jnp.float32),
        lax.psum(g_out_bias.astype(jnp.bfloat16), "dp").astype(jnp.float32),
        lax.psum(g_up.astype(jnp.bfloat16), "dp").astype(jnp.float32),
        lax.psum(g_up_bias.astype(jnp.bfloat16), "dp").astype(jnp.float32),
        lax.psum(g_down.astype(jnp.bfloat16), "dp").astype(jnp.float32),
        lax.psum(g_down_bias.astype(jnp.bfloat16), "dp").astype(jnp.float32),
        lax.psum(g_gain1.astype(jnp.bfloat16), "dp").astype(jnp.float32),
        lax.psum(g_shift1.astype(jnp.bfloat16), "dp").astype(jnp.float32),
        lax.psum(g_gain2.astype(jnp.bfloat16), "dp").astype(jnp.float32),
        lax.psum(g_shift2.astype(jnp.bfloat16), "dp").astype(jnp.float32),
    )
    return (
        mixed,
        d_tokens,
        g_qkv,
        g_bias_q,
        g_bias_v,
        g_out,
        g_out_bias,
        g_up,
        g_up_bias,
        g_down,
        g_down_bias,
        g_gain1,
        g_shift1,
        g_gain2,
        g_shift2,
    )


def solution(mesh):
    placed = (
        P("dp", None),
        P(),
        P("dp"),
        P(None, None, "tensor"),
        P("tensor"),
        P("tensor"),
        P("tensor", None),
        P(),
        P(None, "tensor"),
        P("tensor"),
        P("tensor", None),
        P(),
        P(),
        P(),
        P(),
        P(),
        P("dp", None),
    )
    return jax.shard_map(
        shards,
        mesh=mesh,
        in_specs=placed,
        out_specs=(
            P("dp", None),
            P("dp", None),
            P(None, None, "tensor"),
            P("tensor"),
            P("tensor"),
            P("tensor", None),
            P(),
            P(None, "tensor"),
            P("tensor"),
            P("tensor", None),
            P(),
            P(),
            P(),
            P(),
            P(),
        ),
        check_vma=False,
    )
```

profile of v0, /device:TPU:0, one launch (start us, length us, event | category | flops | bytes accessed | tf_op | source)
XLA Modules:
  0.0 861.5 jit_solution(17869060924698833202)
XLA Ops:
  7.3 2.8 convert_reduce_fusion
  10.2 3.6 fusion.17
  13.8 4.3 fusion.57
  18.1 1.1 slice.23
  19.9 0.6 fusion.51
  20.5 0.7 iota_compare_fusion
  21.2 1.5 fusion.43
  22.7 20.7 %fusion.63 = (f32[5,1536]{1,0:T(8,128)S(1)}, f32[5,1536,1536]{1,2,0:T(8,128)}) fusion(bf16[1536,5,64]{0,2,1:T(8,128)(2,1)} %bitcast.51, bf16[1536,5,64]{0,2,1:T(8,128)(2,1)} %bitcast.55, pred[1536]{0:T(1024)(128)(4,1)S(1)} %iota_compare_fusion), kind=kOutput, calls=%fused_computation.100 | convolution fusion | flops 1545331200 | bytes 49184256 | tf_op jit(solution)/shard_map/while/body/eval_jaxpr/qhe,khe->hqk/dot_general | solution.py:50
  43.4 18.4 %exponential_reduce_fusion = f32[5,1536]{1,0:T(8,128)S(1)} fusion(f32[5,1536,1536]{1,2,0:T(8,128)} %get-tuple-element.108, f32[5,1536]{1,0:T(8,128)S(1)} %get-tuple-element.107), kind=kLoop, calls=%fused_computation.2 | loop fusion | flops 23585280 | bytes 47247360 | tf_op jit(solution)/shard_map/while/body/eval_jaxpr/reduce_sum | solution.py:101
  61.8 17.4 %fusion.39 = bf16[5,64,1536]{2,1,0:T(8,128)(2,1)S(1)} fusion(bf16[1536,5,64]{0,2,1:T(8,128)(2,1)S(1)} %bitcast.53, f32[5,1536,1536]{1,2,0:T(8,128)} %get-tuple-element.108, f32[5,1536]{1,0:T(8,128)S(1)} %log_add_fusion), kind=kOutput, calls=%fused_computation.65 | convolution fusion | flops 1534033920 | bytes 49182720 | tf_op jit(solution)/shard_map/while/body/eval_jaxpr/hqk,khe->qhe/dot_general | solution.py:103
  79.2 0.9 copy-done.15
  80.2 4.2 convolution_convert_fusion.5
  84.4 84.0 %all-reduce.8.cloned.1.call-done = bf16[1536,1280]{1,0:T(8,128)(2,1)} async-done(((bf16[1536,1280]{1,0:T(8,128)(2,1)}), bf16[1536,1280]{1,0:T(8,128)(2,1)}) %all-reduce.8.cloned.1.call-update) | async-done | bytes 3932176 | tf_op jit(solution)/shard_map/psum | solution.py:112
  168.4 4.8 fusion.42
  173.3 0.8 copy-done.7
  174.1 2.8 multiply_reduce_fusion
  176.9 8.8 %multiply_convert_fusion.1 = (bf16[1536,1280]{1,0:T(8,128)(2,1)}, f32[1536,1280]{1,0:T(8,128)S(1)}) fusion(f32[1280]{0:T(1024)S(1)} %copy-done.39, bf16[1280,1280]{1,0:T(8,128)(2,1)S(1)} %copy-done, f32[1280]{0:T(1024)S(1)} %copy-done.40, f32[1280]{0:T(1024)S(1)} %copy-done.31, f32[1536]{0:T(1024)S(1)} %add_rsqrt_fusion, ...), kind=kOutput, calls=%fused_computation.48 | convolution fusion | flops 5062656000 | bytes 22970368 | tf_op jit(solution)/shard_map/dot_general | solution.py:118
  185.7 7.2 fusion.64
  192.9 1.9 copy-done.44
  194.8 6.8 convolution_convert_fusion.3
  201.6 9.6 %convolution_convert_fusion.4 = bf16[1536,1280]{1,0:T(8,128)(2,1)} fusion(bf16[1536,1280]{1,0:T(8,128)(2,1)} %get-tuple-element.109, bf16[1280,1280]{1,0:T(8,128)(2,1)} %param.27), kind=kOutput, calls=%fused_computation.56 | convolution fusion | flops 5035130880 | bytes 11141120 | tf_op jit(solution)/shard_map/dot_general | solution.py:122
  211.3 71.8 %all-reduce.10.cloned.1.call-done = bf16[1536,1280]{1,0:T(8,128)(2,1)} async-done(((bf16[1536,1280]{1,0:T(8,128)(2,1)}), bf16[1536,1280]{1,0:T(8,128)(2,1)}) %all-reduce.10.cloned.1.call-update) | async-done | bytes 3932176 | tf_op jit(solution)/shard_map/psum | solution.py:133
  283.1 9.3 %fusion.22 = (bf16[1280]{0:T(1024)(128)(2,1)S(1)}, f32[1536]{0:T(1024)S(1)}, f32[1536]{0:T(1024)S(1)}) fusion(bf16[1536,1280]{1,0:T(8,128)(2,1)} %all-reduce.10.cloned.1.call-done, f32[1536]{0:T(1024)S(1)} %add_rsqrt_fusion, f32[1536]{0:T(1024)S(1)} %broadcast_multiply_fusion.4, f32[1280]{0:T(1024)S(1)} %copy-done.26, ...), kind=kLoop, calls=%fused_computation.36 | loop fusion | flops 25554688 | bytes 11833856 | tf_op jit(solution)/shard_map/reduce_sum | solution.py:136
  292.4 7.0 fusion.59
  299.4 1.5 convolution_convert_fusion.9
  301.6 1.1 copy-done.6
  302.7 25.4 %multiply_convert_fusion = bf16[5,1536,1536]{1,2,0:T(8,128)(2,1)} fusion(f32[5,1536,1536]{1,2,0:T(8,128)} %get-tuple-element.108, bf16[1536,5,64]{0,2,1:T(8,128)(2,1)S(1)} %bitcast.49, bf16[1536,5,64]{0,2,1:T(8,128)(2,1)S(1)} %bitcast.54, f32[5,1536]{1,0:T(8,128)S(1)} %bitcast.60, f32[5,1536]{1,0:T(8,128)S(1)} %log_add_fusion), kind=kOutput, calls=%fused_computation | convolution fusion | flops 1568931840 | bytes 72806400 | tf_op jit(solution)/shard_map/while/body/eval_jaxpr/qhe,khe->hqk/dot_general | solution.py:149
  328.2 12.9 %fusion.62 = (bf16[5,64]{1,0:T(8,128)(2,1)S(1)}, bf16[1536,5,64]{0,2,1:T(8,128)(2,1)}) fusion(bf16[1536,5,64]{0,2,1:T(8,128)(2,1)S(1)} %bitcast.56, bf16[5,1536,1536]{1,2,0:T(8,128)(2,1)} %multiply_convert_fusion), kind=kOutput, calls=%fused_computation.99 | convolution fusion | flops 1510932224 | bytes 25559680 | tf_op jit(solution)/shard_map/while/body/eval_jaxpr/hqk,khe->qhe/dot_general | solution.py:156
  341.1 11.8 %convolution_convert_fusion.7 = bf16[5,64,1536]{2,1,0:T(8,128)(2,1)S(1)} fusion(bf16[1536,5,64]{0,2,1:T(8,128)(2,1)S(1)} %bitcast.52, bf16[5,1536,1536]{1,2,0:T(8,128)(2,1)} %multiply_convert_fusion), kind=kOutput, calls=%fused_computation.66 | convolution fusion | flops 1510440960 | bytes 25559040 | tf_op jit(solution)/shard_map/while/body/eval_jaxpr/hqk,qhe->khe/dot_general | solution.py:159
  352.9 17.4 %fusion.61 = (bf16[5,64]{1,0:T(8,128)(2,1)S(1)}, bf16[1536,5,64]{0,2,1:T(8,128)(2,1)S(1)}) fusion(bf16[1536,5,64]{0,2,1:T(8,128)(2,1)S(1)} %bitcast.50, f32[5,1536,1536]{1,2,0:T(8,128)} %get-tuple-element.108, f32[5,1536]{1,0:T(8,128)S(1)} %log_add_fusion), kind=kOutput, calls=%fused_computation.98 | convolution fusion | flops 1534525184 | bytes 49183360 | tf_op jit(solution)/shard_map/while/body/eval_jaxpr/hqk,qhe->khe/dot_general | solution.py:162
  370.4 0.9 copy-done.20
  371.3 8.3 convolution_convert_fusion
  379.7 10.0 %convolution_convert_fusion.1 = bf16[1280,1280]{1,0:T(8,128)(2,1)} fusion(bf16[1536,1280]{1,0:T(8,128)(2,1)} %get-tuple-element.109, bf16[1536,1280]{1,0:T(8,128)(2,1)} %param.33, pred[1536]{0:T(1024)(128)(4,1)S(1)} %iota_compare_fusion), kind=kOutput, calls=%fused_computation.53 | convolution fusion | flops 5040701440 | bytes 11142656 | tf_op jit(solution)/shard_map/dot_general | solution.py:37
  389.7 8.0 convolution_convert_fusion.2
  397.8 2.4 convolution_convert_fusion.8
  400.3 5.8 convolution_convert_fusion.6
  406.3 2.7 reduce_sum.207
  409.0 116.2 %all-reduce.14.cloned.1.call-done = (bf16[1536,1280]{1,0:T(8,128)(2,1)}, bf16[1536,1280]{1,0:T(8,128)(2,1)}) async-done(((bf16[1536,1280]{1,0:T(8,128)(2,1)}, bf16[1536,1280]{1,0:T(8,128)(2,1)}), (bf16[1536,1280]{1,0:T(8,128)(2,1)}, bf16[1536,1280]{1,0:T(8,128)(2,1)})) %all-reduce.14.cloned.1.call-update) | async-done | bytes 7864336 | tf_op jit(solution)/shard_map/psum | solution.py:121
  525.2 2.7 reduce_sum.205
  528.0 6.1 fusion.24
  534.1 39.1 %all-reduce = (bf16[320]{0:T(512)(128)(2,1)S(1)}, bf16[320]{0:T(512)(128)(2,1)S(1)}, bf16[1280]{0:T(1024)(128)(2,1)S(1)}, bf16[1280]{0:T(1024)(128)(2,1)S(1)}, b...) all-reduce(bf16[320]{0:T(512)(128)(2,1)S(1)} %convert_element_type., ...), channel_id=1, replica_groups=mesh['dp'=8,'tensor'=4] {'dp'}, use_global_device_ids=true, to_apply=%region_18.19 | all-reduce | flops 9600 | bytes 38400 | tf_op jit(solution)/shard_map/psum | solution.py:211
  573.2 0.6 convert_element_type.235
  578.6 15.5 %fusion.16 = (f32[1536,1280]{1,0:T(8,128)}, bf16[1536,1280]{1,0:T(8,128)(2,1)}) fusion(f32[1536,1280]{1,0:T(8,128)} %copy-done.6, bf16[1536,1280]{1,0:T(8,128)(2,1)} %param.17, bf16[1536,1280]{1,0:T(8,128)(2,1)} %get-tuple-element.95, f32[1536]{0:T(1024)S(1)} %broadcast_multiply_fusion, f32[1536]{0:T(1024)S(1)} %broadcast_multiply_fusion.1, ...), kind=kLoop, calls=%fused_computation.30 | loop fusion | flops 37355520 | bytes 35430912 | tf_op jit(solution)/shard_map/jit(_where)/select_n | solution.py:194
  594.1 247.8 %all-reduce.12.cloned.1.call-done = (bf16[1280,3,320]{0,2,1:T(8,128)(2,1)}, bf16[320,1280]{1,0:T(8,128)(2,1)}, bf16[1280,1280]{1,0:T(8,128)(2,1)}, bf16[1280,1280]{1,0:T(8,128)(2,1)}) async-done(((bf16[1280,3,320]{0,2,1:T(8,128)(2,1)}, bf16[320,1280]{1,0:T(8,128)(2,1)}, bf16[1280,1280]{1,0:T(8,128)(2,1)}, bf16[1280,1280]{1,0:T(8,128)(2,1)}), (bf16[1280,3,320]{0,2,1:T(8,128)(2,1)}, ...) | async-done | bytes 9830416 | tf_op jit(solution)/shard_map/psum | solution.py:210
  841.9 5.4 convert_element_type.237
  847.2 3.5 convert_element_type.241
  850.8 2.7 convert_element_type.225
  853.4 1.3 convert_element_type.233
  (119 shorter events, 6.2 us)
Async XLA Ops:
  7.2 169.6 %copy-start = (bf16[1280,1280]{1,0:T(8,128)(2,1)S(1)}, bf16[1280,1280]{1,0:T(8,128)(2,1)}, u32[]{:S(2)}) copy-start(bf16[1280,1280]{1,0:T(8,128)(2,1)} %param.25) | copy-start | bytes 9830404
  7.2 6.6 copy-start.32
  7.2 6.6 copy-start.41
  7.2 161.2 %all-reduce.8.cloned.1.call-start = ((), (), s32[]{:S(2)}) async-start(), calls=%async_computation | async-start | bytes 7864320 | tf_op jit(solution)/shard_map/psum | solution.py:112
  7.3 6.5 copy-start.2
  7.3 6.5 copy-start.38
  10.2 8.0 copy-start.27
  13.7 4.4 copy-start.29
  13.8 6.1 copy-start.43
  13.8 7.4 copy-start.35
  13.8 7.4 copy-start.36
  43.4 18.4 %copy-start.12 = (bf16[1536,320]{0,1:T(8,128)(2,1)S(1)}, bf16[1536,320]{0,1:T(8,128)(2,1)}, u32[]{:S(2)}) copy-start(bf16[1536,320]{0,1:T(8,128)(2,1)} %get-tuple-element.99) | copy-start | bytes 2949124
  61.8 18.4 %copy-start.24 = (bf16[320,1280]{1,0:T(8,128)(2,1)S(1)}, bf16[320,1280]{1,0:T(8,128)(2,1)}, u32[]{:S(2)}) copy-start(bf16[320,1280]{1,0:T(8,128)(2,1)} %param.23) | copy-start | bytes 2457604
  79.2 89.2 %copy-start.26 = (f32[1280]{0:T(1024)S(1)}, f32[1280]{0:T(1024)}, u32[]{:S(2)}) copy-start(f32[1280]{0:T(1024)} %param.24) | copy-start | bytes 15364
  84.3 92.5 %copy-start.31 = (f32[1280]{0:T(1024)S(1)}, f32[1280]{0:T(1024)}, u32[]{:S(2)}) copy-start(f32[1280]{0:T(1024)} %param.31) | copy-start | bytes 15364
  84.4 92.5 %copy-start.39 = (f32[1280]{0:T(1024)S(1)}, f32[1280]{0:T(1024)}, u32[]{:S(2)}) copy-start(f32[1280]{0:T(1024)} %param.26) | copy-start | bytes 15364
  84.4 92.5 %copy-start.40 = (f32[1280]{0:T(1024)S(1)}, f32[1280]{0:T(1024)}, u32[]{:S(2)}) copy-start(f32[1280]{0:T(1024)} %param.32) | copy-start | bytes 15364
  84.4 198.7 %all-reduce.10.cloned.1.call-start = ((), (), s32[]{:S(2)}) async-start(), calls=%async_computation.1 | async-start | bytes 7864320 | tf_op jit(solution)/shard_map/psum | solution.py:133
  168.4 4.8 copy-start.3
  168.4 5.6 copy-start.7
  176.9 8.8 %copy-start.17 = (bf16[1536,1280]{1,0:T(8,128)(2,1)S(1)}, bf16[1536,1280]{1,0:T(8,128)(2,1)}, u32[]{:S(2)}) copy-start(bf16[1536,1280]{1,0:T(8,128)(2,1)} %param.33) | copy-start | bytes 11796484
  176.9 8.8 %copy-start.37 = (bf16[1280,1280]{1,0:T(8,128)(2,1)S(1)}, bf16[1280,1280]{1,0:T(8,128)(2,1)}, u32[]{:S(2)}) copy-start(bf16[1280,1280]{1,0:T(8,128)(2,1)} %param.27) | copy-start | bytes 9830404
  201.6 323.7 %all-reduce.14.cloned.1.call-start = ((), (), s32[]{:S(2)}) async-start(), calls=%async_computation.3 | async-start | bytes 15728640 | tf_op jit(solution)/shard_map/psum | solution.py:121
  283.1 9.3 %copy-start.4 = (bf16[1536,1280]{1,0:T(8,128)(2,1)S(1)}, bf16[1536,1280]{1,0:T(8,128)(2,1)}, u32[]{:S(2)}) copy-start(bf16[1536,1280]{1,0:T(8,128)(2,1)} %param.17) | copy-start | bytes 11796484
  283.1 9.3 %copy-start.8 = (bf16[1536,1280]{1,0:T(8,128)(2,1)S(1)}, bf16[1536,1280]{1,0:T(8,128)(2,1)}, u32[]{:S(2)}) copy-start(bf16[1536,1280]{1,0:T(8,128)(2,1)} %all-reduce.8.cloned.1.call-done) | copy-start | bytes 11796484
  283.1 9.3 %copy-start.10 = (bf16[1536,1280]{1,0:T(8,128)(2,1)S(1)}, bf16[1536,1280]{1,0:T(8,128)(2,1)}, u32[]{:S(2)}) copy-start(bf16[1536,1280]{1,0:T(8,128)(2,1)} %all-reduce.10.cloned.1.call-done) | copy-start | bytes 11796484
  292.4 7.0 copy-start.25
  299.4 3.3 copy-start.6
  299.4 3.3 copy-start.13
  302.7 25.5 %copy-start.14 = (bf16[1536,320]{0,1:T(8,128)(2,1)S(1)}, bf16[1536,320]{0,1:T(8,128)(2,1)}, u32[]{:S(2)}) copy-start(bf16[1536,320]{0,1:T(8,128)(2,1)} %slice.23) | copy-start | bytes 2949124
  328.2 13.0 %copy-start.11 = (bf16[1536,320]{0,1:T(8,128)(2,1)S(1)}, bf16[1536,320]{0,1:T(8,128)(2,1)}, u32[]{:S(2)}) copy-start(bf16[1536,320]{0,1:T(8,128)(2,1)} %get-tuple-element.98) | copy-start | bytes 2949124
  379.6 462.3 %all-reduce.12.cloned.1.call-start = ((), (), s32[]{:S(2)}) async-start(), calls=%async_computation.2 | async-start | bytes 19660800 | tf_op jit(solution)/shard_map/psum | solution.py:210
  379.7 10.0 %copy-start.5 = (bf16[1536,1280]{1,0:T(8,128)(2,1)S(1)}, bf16[1536,1280]{1,0:T(8,128)(2,1)}, u32[]{:S(2)}) copy-start(bf16[1536,1280]{1,0:T(8,128)(2,1)} %param.17) | copy-start | bytes 11796484
  379.7 10.0 %copy-start.9 = (bf16[1536,1280]{1,0:T(8,128)(2,1)S(1)}, bf16[1536,1280]{1,0:T(8,128)(2,1)}, u32[]{:S(2)}) copy-start(bf16[1536,1280]{1,0:T(8,128)(2,1)} %all-reduce.8.cloned.1.call-done) | copy-start | bytes 11796484
  379.7 10.0 %copy-start.45 = (bf16[1536,1280]{1,0:T(8,128)(2,1)S(1)}, bf16[1536,1280]{1,0:T(8,128)(2,1)}, u32[]{:S(2)}) copy-start(bf16[1536,1280]{1,0:T(8,128)(2,1)} %copy-done.44) | copy-start | bytes 11796484
  379.7 18.0 %slice-start = ((s8[7864320]{0:T(1024)(128)(4,1)}), s8[4194304]{0:T(1024)(128)(4,1)S(1)}, s32[]{:S(2)}) async-start(s8[7864320]{0:T(1024)(128)(4,1)} %bitcast.46), calls=%async_computation.4 | async-start | bytes 8388608
  389.7 8.0 slice-start.1
  397.7 2.5 copy-start.21
  397.7 2.5 copy-start.22
  397.7 2.5 copy-start.28
  397.7 2.5 copy-start.30
  397.8 2.5 copy-start.33
  397.8 2.5 copy-start.42
  406.3 172.3 %copy-start.34 = (f32[1280]{0:T(1024)S(1)}, f32[1280]{0:T(1024)}, u32[]{:S(2)}) copy-start(f32[1280]{0:T(1024)} %param.28) | copy-start | bytes 15364
  841.9 5.4 copy-start.18
  841.9 8.9 %copy-start.19 = (bf16[1280,3,320]{0,2,1:T(8,128)(2,1)S(1)}, bf16[1280,3,320]{0,2,1:T(8,128)(2,1)}, u32[]{:S(2)}) copy-start(bf16[1280,3,320]{0,2,1:T(8,128)(2,1)} %get-tuple-element.90) | copy-start | bytes 7372804
  847.2 7.5 copy-start.1
  847.2 6.2 copy-start.23
  (4 other events, 5.7 us)
Sparse Core Ops, SparseCore 0:
  84.5 83.9 all-reduce.7
  201.7 81.3 all-reduce.9
  379.7 145.4 all-reduce.13
  530.1 311.6 all-reduce.11
where the time goes:
time: 867 us; the launch traced here: 862 us
  waiting for transfers between devices  520 us (60%)
  matrix products  182 us (21%)
  other arithmetic  97 us (11%)
  blocking collectives  39.1 us (5%)
  between operations  15.3 us (2%)
    psum x1, waiting for transfers between devices, shards(): lax.psum(g_qkv.astype(jnp.bfloat16), 'dp').astype(jnp.float32)  248 us
    psum x1, waiting for transfers between devices, shards(): lax.psum(jnp.dot(hidden, w_down, preferred_element_type=jnp.float32).asty...  116 us
    psum x1, waiting for transfers between devices, shards(): lax.psum(jnp.dot(context, w_out, preferred_element_type=jnp.float32).asty...  84 us
    psum x1, waiting for transfers between devices, shards(): lax.psum(contract_last(d_pre_b, w_up).astype(jnp.bfloat16), 'tensor')  71.8 us
    psum x1, blocking collectives, shards(): lax.psum(g_bias_q.astype(jnp.bfloat16), 'dp').astype(jnp.float32)  39.1 us
    dot_general x4, matrix products, contract_first(): lax.dot_general(left, right, (((0,), (0,)), ((), ())), preferred_element_...  26.2 us
    dot_general x1, matrix products, backward_clip(): jnp.einsum('qhe,khe->hqk', dcontext_clip, values_clip, preferred_element_...  25.4 us
    dot_general x4, matrix products, contract_last(): lax.dot_general(left, right, (((1,), (1,)), ((), ())), preferred_element_...  23.7 us
  transfers between devices with their start and end apart: 4, of which 4 were waited for; matrix products, arithmetic and copies ran while one was open for 8% of the time, Pallas kernels for 0%

commit v1 on v0

--- a/solution.py
+++ b/solution.py
@@ -1,6 +1,10 @@
+import functools
+
 import jax
 import jax.numpy as jnp
 from jax import lax
+from jax.experimental import pallas as pl
+from jax.experimental.pallas import tpu as pltpu
 from jax.sharding import PartitionSpec as P
 
 HD = 64
@@ -53,7 +57,7 @@
     return jnp.where((positions < length)[None, None, :], raw, NEG)
 
 
-def shards(
+def plain(
     tokens,
     clip_len,
     slot_clip,
@@ -240,6 +244,845 @@
     )
 
 
+MESH = pl.DeviceIdType.MESH
+DMA = pltpu.SemaphoreType.DMA
+ANY = pl.BlockSpec(memory_space=pl.ANY)
+VMEM = pl.BlockSpec(memory_space=pltpu.VMEM)
+SMEM = pl.BlockSpec(memory_space=pltpu.SMEM)
+BLOCKS = (96,)
+BQ = 256
+BK = 256
+
+
+def coords():
+    dp = lax.axis_index("dp")
+    t = lax.axis_index("tensor")
+    return dp // 2, dp % 2, t // 2, t % 2
+
+
+def device(z, y, x, c):
+    return (z * 2 + y, x * 2 + c)
+
+
+def greet(peers):
+    barrier = pltpu.get_barrier_semaphore()
+    for peer in peers:
+        pl.semaphore_signal(barrier, inc=1, device_id=peer, device_id_type=MESH)
+    pl.semaphore_wait(barrier, len(peers))
+
+
+def greet_grid():
+    z, y, x, c = coords()
+    barrier = pltpu.get_barrier_semaphore()
+
+    def signal(peer):
+        pl.semaphore_signal(barrier, inc=1, device_id=peer, device_id_type=MESH)
+
+    @pl.when(z > 0)
+    def _():
+        signal(device(z - 1, y, x, c))
+
+    @pl.when(z < 3)
+    def _():
+        signal(device(z + 1, y, x, c))
+
+    signal(device(z, 1 - y, x, c))
+    signal(device(z, y, 1 - x, c))
+    signal(device(z, y, x, 1 - c))
+
+    pl.semaphore_wait(barrier, 3 + jnp.minimum(z, 1) + jnp.minimum(3 - z, 1))
+
+
+GATHER_SEMS = [DMA, DMA((4,)), DMA((4,)), DMA((4,)), DMA((8,)), DMA((16,)), DMA((32,))]
+
+
+def gather_steps(x_ref, o_ref, local_sem, right_sem, left_sem, u_sem, v_sem, core_sem, recv_sem):
+    z, y, x, c = coords()
+    size = x_ref.shape[0]
+
+    def block(z, y, x, c):
+        return (z * 2 + y) * 4 + x * 2 + c
+
+    def rows(b):
+        return o_ref.at[pl.ds(pl.multiple_of(b * size, size), size)]
+
+    ux, uy = x + (1 - c) * (1 - 2 * x), y + c * (1 - 2 * y)
+    vx, vy = x + c * (1 - 2 * x), y + (1 - c) * (1 - 2 * y)
+
+    def copy(b, src, sem, peer):
+        return pltpu.make_async_remote_copy(
+            src_ref=src,
+            dst_ref=rows(b),
+            send_sem=sem,
+            recv_sem=recv_sem.at[b],
+            device_id=peer,
+            device_id_type=MESH,
+        )
+
+    def send_right(b, src, i):
+        copy(b, src, right_sem.at[i], device(z + 1, y, x, c)).start()
+
+    def send_left(b, src, i):
+        copy(b, src, left_sem.at[i], device(z - 1, y, x, c)).start()
+
+    def send_u(b, src, i):
+        copy(b, src, u_sem.at[i], device(z, uy, ux, c)).start()
+
+    def send_v(b, src, i):
+        copy(b, src, v_sem.at[i], device(z, vy, vx, c)).start()
+
+    def send_core(b, src, i):
+        copy(b, src, core_sem.at[i], device(z, y, x, 1 - c)).start()
+
+    def arrived(b):
+        copy(b, x_ref, core_sem.at[0], device(z, y, x, 1 - c)).wait_recv()
+
+    own = block(z, y, x, c)
+    local = pltpu.make_async_copy(x_ref, rows(own), local_sem)
+    local.start()
+
+    @pl.when(z < 3)
+    def _():
+        send_right(own, x_ref, z)
+
+    @pl.when(z > 0)
+    def _():
+        send_left(own, x_ref, z)
+
+    send_u(own, x_ref, z)
+    send_v(own, x_ref, z)
+    send_core(own, x_ref, z)
+
+    def got_line(at):
+        b = block(at, y, x, c)
+        arrived(b)
+
+        @pl.when((at < z) & (z < 3))
+        def _():
+            send_right(b, rows(b), at)
+
+        @pl.when((at > z) & (z > 0))
+        def _():
+            send_left(b, rows(b), at)
+
+        send_u(b, rows(b), at)
+        send_v(b, rows(b), at)
+        send_core(b, rows(b), at)
+
+    def got_u(at):
+        b = block(at, uy, ux, c)
+        arrived(b)
+        send_v(b, rows(b), 4 + at)
+        send_core(b, rows(b), 4 + at)
+
+    def got_v(at):
+        b = block(at, vy, vx, c)
+        arrived(b)
+        send_core(b, rows(b), 8 + at)
+
+    def got_uv(at):
+        b = block(at, 1 - y, 1 - x, c)
+        arrived(b)
+        send_core(b, rows(b), 12 + at)
+
+    def around(step, distance):
+        for side in (-1, 1) if distance else (0,):
+            at = z + side * distance
+            pl.when((at >= 0) & (at < 4))(functools.partial(step, at))
+
+    for distance in range(4):
+        if distance:
+            around(got_line, distance)
+        around(got_u, distance)
+    for distance in range(4):
+        around(got_v, distance)
+        around(got_uv, distance)
+
+    @pl.loop(0, 16)
+    def _(i):
+        arrived((i // 2) * 4 + (i % 2) * 2 + 1 - c)
+
+    local.wait()
+
+    def sent(sem):
+        copy(own, x_ref, sem, device(z, y, x, 1 - c)).wait_send()
+
+    @pl.loop(0, 16)
+    def _(i):
+        sent(core_sem.at[i])
+
+    @pl.loop(0, 8)
+    def _(i):
+        sent(v_sem.at[i])
+
+    @pl.loop(0, 4)
+    def _(i):
+        sent(u_sem.at[i])
+
+        @pl.when((i <= z) & (z < 3))
+        def _():
+            sent(right_sem.at[i])
+
+        @pl.when((i >= z) & (z > 0))
+        def _():
+            sent(left_sem.at[i])
+
+
+def gather_kernel(*refs):
+    greet_grid()
+    n = len(GATHER_SEMS)
+    arrays = len(refs) // (n + 2)
+    for a in range(arrays):
+        gather_steps(refs[a], refs[arrays + a], *refs[2 * arrays + a * n : 2 * arrays + (a + 1) * n])
+
+
+def gather32(arrays, spare, cid):
+    return pl.pallas_call(
+        gather_kernel,
+        out_shape=[
+            jax.ShapeDtypeStruct((32 * a.shape[0] + e, a.shape[1]), a.dtype)
+            for a, e in zip(arrays, spare)
+        ],
+        in_specs=[ANY] * len(arrays),
+        out_specs=[ANY] * len(arrays),
+        scratch_shapes=GATHER_SEMS * len(arrays),
+        compiler_params=pltpu.CompilerParams(collective_id=cid, has_side_effects=True),
+        name="gather32",
+    )(*arrays)
+
+
+def table_kernel(x_ref, o_ref, send_sem, recv_sem):
+    me = lax.axis_index("dp")
+    t = lax.axis_index("tensor")
+    peers = [(lax.rem(me + s, 8), t) for s in range(1, 8)]
+    greet(peers)
+    o_ref[me] = x_ref[...]
+    copies = [
+        pltpu.make_async_remote_copy(
+            src_ref=x_ref,
+            dst_ref=o_ref.at[me],
+            send_sem=send_sem.at[s],
+            recv_sem=recv_sem.at[s],
+            device_id=peer,
+            device_id_type=MESH,
+        )
+        for s, peer in enumerate(peers)
+    ]
+    for copy in copies:
+        copy.start()
+    for copy in copies:
+        copy.wait()
+
+
+def gather_table(value, cid):
+    tile = jnp.broadcast_to(value.reshape(1, 1), (8, 128))
+    out = pl.pallas_call(
+        table_kernel,
+        out_shape=jax.ShapeDtypeStruct((8, 8, 128), value.dtype),
+        in_specs=[VMEM],
+        out_specs=VMEM,
+        scratch_shapes=[DMA((7,)), DMA((7,))],
+        compiler_params=pltpu.CompilerParams(collective_id=cid, has_side_effects=True),
+        name="table",
+    )(tile)
+    return out[:, 0, 0]
+
+
+def pieces_kernel(size, info_ref, x_ref, u_ref, xo_ref, uo_ref, held, sems):
+    t = lax.axis_index("tensor")
+    cap = x_ref.shape[0]
+    offset = info_ref[0]
+    length = info_ref[1]
+    loads = [
+        pltpu.make_async_copy(src, held.at[i, pl.ds(size, cap)], sems.at[i])
+        for i, src in enumerate((x_ref, u_ref))
+    ]
+    for load in loads:
+        load.start()
+    for i in (0, 1):
+        held[i, 0:size, :] = jnp.zeros((size, held.shape[2]), held.dtype)
+        held[i, size + cap :, :] = jnp.zeros((size, held.shape[2]), held.dtype)
+    for i, out in enumerate((xo_ref, uo_ref)):
+        loads[i].wait()
+
+        @pl.loop(0, 8)
+        def _(b):
+            first = (b * 4 + t) * size - offset + size
+            first = pl.multiple_of(jnp.clip(first, 0, cap + size), 16)
+            row = lax.broadcasted_iota(jnp.int32, (size, 1), 0) + first - size
+            value = held[i, pl.ds(first, size), :].astype(jnp.float32)
+            value = jnp.where((row >= 0) & (row < length), value, 0.0)
+            out[b] = value.astype(jnp.bfloat16)
+
+
+def take_pieces(x, u, info, size):
+    cap, width = x.shape
+    shape = jax.ShapeDtypeStruct((8, size, width), jnp.bfloat16)
+    return pl.pallas_call(
+        functools.partial(pieces_kernel, size),
+        out_shape=(shape, shape),
+        in_specs=[SMEM, ANY, ANY],
+        out_specs=(VMEM, VMEM),
+        scratch_shapes=[pltpu.VMEM((2, cap + 2 * size, width), jnp.bfloat16), DMA((2,))],
+        compiler_params=pltpu.CompilerParams(vmem_limit_bytes=40 << 20),
+        name="pieces",
+    )(info, x, u)
+
+
+def pack_kernel(
+    p_ref,
+    o_ref,
+    acc,
+    own,
+    y_out,
+    y_in,
+    r_out,
+    r_in,
+    l_out,
+    l_in,
+    ys,
+    yr,
+    rs,
+    rr,
+    ls,
+    lr,
+    *gather_sems,
+):
+    z, y, x, c = coords()
+    greet_grid()
+
+    def piece(zp, yp):
+        return p_ref[zp * 2 + yp].astype(jnp.float32)
+
+    def y_copy(i):
+        return pltpu.make_async_remote_copy(
+            src_ref=y_out.at[i],
+            dst_ref=y_in.at[i],
+            send_sem=ys.at[i],
+            recv_sem=yr.at[i],
+            device_id=device(z, 1 - y, x, c),
+            device_id_type=MESH,
+        )
+
+    def r_copy(i):
+        return pltpu.make_async_remote_copy(
+            src_ref=r_out.at[i],
+            dst_ref=r_in.at[i],
+            send_sem=rs.at[i],
+            recv_sem=rr.at[i],
+            device_id=device(z + 1, y, x, c),
+            device_id_type=MESH,
+        )
+
+    def l_copy(i):
+        return pltpu.make_async_remote_copy(
+            src_ref=l_out.at[i],
+            dst_ref=l_in.at[i],
+            send_sem=ls.at[i],
+            recv_sem=lr.at[i],
+            device_id=device(z - 1, y, x, c),
+            device_id_type=MESH,
+        )
+
+    def add(ref, copy, i):
+        copy(i).wait_recv()
+        acc[...] += ref[i].astype(jnp.float32)
+
+    def flow(zp, yp, first):
+        i = zp * 2 + yp
+
+        @pl.when(z < zp)
+        def _():
+            first()
+
+            @pl.when(z > 0)
+            def _():
+                add(r_in, r_copy, i)
+
+            r_out[i] = acc[...].astype(jnp.bfloat16)
+            r_copy(i).start()
+
+        @pl.when(z > zp)
+        def _():
+            first()
+
+            @pl.when(z < 3)
+            def _():
+                add(l_in, l_copy, i)
+
+            l_out[i] = acc[...].astype(jnp.bfloat16)
+            l_copy(i).start()
+
+    def land(yp):
+        @pl.when(z > 0)
+        def _():
+            add(r_in, r_copy, z * 2 + yp)
+
+        @pl.when(z < 3)
+        def _():
+            add(l_in, l_copy, z * 2 + yp)
+
+    order = (0, 3, 1, 2)
+
+    @pl.when(c == 0)
+    def _():
+        for zp in order:
+            y_out[zp] = piece(zp, 1 - y).astype(jnp.bfloat16)
+            y_copy(zp).start()
+        for zp in order:
+
+            def first(zp=zp):
+                acc[...] = piece(zp, y)
+                add(y_in, y_copy, zp)
+
+            flow(zp, y, first)
+        acc[...] = piece(z, y)
+        add(y_in, y_copy, z)
+        land(y)
+        own[...] = acc[...].astype(jnp.bfloat16)
+        for zp in order:
+            y_copy(zp).wait_send()
+
+    @pl.when(c == 1)
+    def _():
+        for zp in order:
+            for yp in (0, 1):
+
+                def first(zp=zp, yp=yp):
+                    acc[...] = piece(zp, yp)
+
+                flow(zp, yp, first)
+        acc[...] = piece(z, 1 - y)
+        land(1 - y)
+        y_out[0] = acc[...].astype(jnp.bfloat16)
+        y_copy(0).start()
+        acc[...] = piece(z, y)
+        land(y)
+        add(y_in, y_copy, 0)
+        own[...] = acc[...].astype(jnp.bfloat16)
+        y_copy(0).wait_send()
+
+    for zp in range(4):
+        for yp in (0, 1):
+            used = (c == 1) | (y == yp)
+
+            @pl.when(used & (z < zp))
+            def _(i=zp * 2 + yp):
+                r_copy(i).wait_send()
+
+            @pl.when(used & (z > zp))
+            def _(i=zp * 2 + yp):
+                l_copy(i).wait_send()
+
+    gather_steps(own, o_ref, *gather_sems)
+
+
+def pack_gather(parts, cid):
+    _, size, width = parts.shape
+    bf16 = jnp.bfloat16
+    slots = pltpu.VMEM((8, size, width), bf16)
+    quarter = pltpu.VMEM((4, size, width), bf16)
+    return pl.pallas_call(
+        pack_kernel,
+        out_shape=jax.ShapeDtypeStruct((32 * size, width), bf16),
+        in_specs=[VMEM],
+        out_specs=ANY,
+        scratch_shapes=[
+            pltpu.VMEM((size, width), jnp.float32),
+            pltpu.VMEM((size, width), bf16),
+            quarter,
+            quarter,
+            slots,
+            slots,
+            slots,
+            slots,
+            DMA((4,)),
+            DMA((4,)),
+            DMA((8,)),
+            DMA((8,)),
+            DMA((8,)),
+            DMA((8,)),
+        ]
+        + GATHER_SEMS,
+        compiler_params=pltpu.CompilerParams(
+            collective_id=cid, has_side_effects=True, vmem_limit_bytes=40 << 20
+        ),
+        name="pack_gather",
+    )(parts)
+
+
+def share_kernel(p_ref, o_ref, landed, send_sem, recv_sem):
+    dp = lax.axis_index("dp")
+    t = lax.axis_index("tensor")
+    peers = [lax.rem(t + s, 4) for s in (2, 3, 1)]
+    greet([(dp, peer) for peer in peers])
+    copies = [
+        pltpu.make_async_remote_copy(
+            src_ref=p_ref.at[peer],
+            dst_ref=landed.at[s],
+            send_sem=send_sem.at[s],
+            recv_sem=recv_sem.at[s],
+            device_id=(dp, peer),
+            device_id_type=MESH,
+        )
+        for s, peer in enumerate(peers)
+    ]
+    for copy in copies:
+        copy.start()
+    total = p_ref[t].astype(jnp.float32)
+    for s, copy in enumerate(copies):
+        copy.wait_recv()
+        total += landed[s].astype(jnp.float32)
+    o_ref[...] = total
+    for copy in copies:
+        copy.wait_send()
+
+
+def share4(parts, cid):
+    rows, width = parts.shape
+    size = rows // 4
+    return pl.pallas_call(
+        share_kernel,
+        out_shape=jax.ShapeDtypeStruct((size, width), jnp.float32),
+        in_specs=[VMEM],
+        out_specs=VMEM,
+        scratch_shapes=[pltpu.VMEM((3, size, width), parts.dtype), DMA((3,)), DMA((3,))],
+        compiler_params=pltpu.CompilerParams(
+            collective_id=cid, has_side_effects=True, vmem_limit_bytes=24 << 20
+        ),
+        name="share4",
+    )(parts.reshape(4, size, width))
+
+
+def dot_nt(a, b):
+    return lax.dot_general(a, b, (((1,), (1,)), ((), ())), preferred_element_type=jnp.float32)
+
+
+def dot_nn(a, b):
+    return lax.dot_general(a, b, (((1,), (0,)), ((), ())), preferred_element_type=jnp.float32)
+
+
+def attend_kernel(heads, klo, khi, qkv_ref, vt_ref, seg_ref, ctx_ref, lse_ref, m_s, l_s, acc_s):
+    i = pl.program_id(0)
+    q0 = pl.multiple_of(i * BQ, BQ)
+    local = heads * HD
+    span = range(heads)
+    start = seg_ref[0:1, pl.ds(q0, BQ)]
+    end = seg_ref[1:2, pl.ds(q0, BQ)]
+    m_s[...] = jnp.full_like(m_s, NEG)
+    l_s[...] = jnp.zeros_like(l_s)
+    acc_s[...] = jnp.zeros_like(acc_s)
+    q = [qkv_ref[pl.ds(q0, BQ), h * HD : (h + 1) * HD] for h in span]
+
+    def body(kb, carry):
+        k0 = pl.multiple_of(kb * BK, BK)
+        key = lax.broadcasted_iota(jnp.int32, (BK, BQ), 0) + k0
+        mask = (key >= start) & (key < end)
+        s = [
+            jnp.where(
+                mask,
+                dot_nt(qkv_ref[pl.ds(k0, BK), local + h * HD : local + (h + 1) * HD], q[h]),
+                NEG,
+            )
+            for h in span
+        ]
+        p, a = [], []
+        for h in span:
+            old = m_s[h]
+            new = jnp.maximum(old, jnp.max(s[h], 0, keepdims=True))
+            e = jnp.exp(s[h] - new)
+            scale = jnp.exp(old - new)
+            l_s[h] = scale * l_s[h] + jnp.sum(e, 0, keepdims=True)
+            m_s[h] = new
+            p.append(e.astype(jnp.bfloat16))
+            a.append(scale)
+        for h in span:
+            vt = vt_ref[h * HD : (h + 1) * HD, pl.ds(k0, BK)]
+            acc_s[h] = a[h] * acc_s[h] + dot_nn(vt, p[h])
+        return carry
+
+    lax.fori_loop(klo[i], khi[i], body, 0)
+    for h in span:
+        total = l_s[h]
+        total = jnp.where(total == 0.0, 1.0, total)
+        lse_ref[h : h + 1, :] = m_s[h] + jnp.log(total)
+        out = acc_s[h] * (1.0 / total)
+        ctx_ref[:, h * HD : (h + 1) * HD] = out.T.astype(jnp.bfloat16)
+
+
+def whole(a):
+    return pl.BlockSpec(a.shape, lambda i, *_: (0,) * len(a.shape), pipeline_mode=pl.Buffered(1))
+
+
+def attend(qkv, vt, seg, klo, khi, heads):
+    rows = qkv.shape[0]
+    local = heads * HD
+    row = pltpu.VMEM((heads, 1, BQ), jnp.float32)
+    return pl.pallas_call(
+        functools.partial(attend_kernel, heads),
+        out_shape=(
+            jax.ShapeDtypeStruct((rows, local), jnp.bfloat16),
+            jax.ShapeDtypeStruct((8, rows), jnp.float32),
+        ),
+        grid_spec=pltpu.PrefetchScalarGridSpec(
+            num_scalar_prefetch=2,
+            grid=(rows // BQ,),
+            in_specs=[whole(qkv), whole(vt), whole(seg)],
+            out_specs=[
+                pl.BlockSpec((BQ, local), lambda i, *_: (i, 0)),
+                pl.BlockSpec((8, BQ), lambda i, *_: (0, i)),
+            ],
+            scratch_shapes=[row, row, pltpu.VMEM((heads, HD, BQ), jnp.float32)],
+        ),
+        compiler_params=pltpu.CompilerParams(vmem_limit_bytes=40 << 20),
+        name="attend",
+    )(klo, khi, qkv, vt, seg)
+
+
+def attend_back_kernel(
+    heads, klo, khi, qkv_ref, kt_ref, do_ref, ctx_ref, lse_ref, seg_ref, d_ref, dbq_ref, dbv_ref, dk_s, dv_s, dq_s
+):
+    i = pl.program_id(0)
+    n = pl.num_programs(0)
+    q0 = pl.multiple_of(i * BQ, BQ)
+    local = heads * HD
+    span = range(heads)
+
+    @pl.when(i == 0)
+    def _():
+        dk_s[...] = jnp.zeros_like(dk_s)
+        dv_s[...] = jnp.zeros_like(dv_s)
+        dbq_ref[...] = jnp.zeros_like(dbq_ref)
+        dbv_ref[...] = jnp.zeros_like(dbv_ref)
+
+    start = seg_ref[0:1, pl.ds(q0, BQ)]
+    end = seg_ref[1:2, pl.ds(q0, BQ)]
+    dq_s[...] = jnp.zeros_like(dq_s)
+    delta = []
+    for h in span:
+        sl = slice(h * HD, (h + 1) * HD)
+        both = do_ref[pl.ds(q0, BQ), sl].astype(jnp.float32) * ctx_ref[pl.ds(q0, BQ), sl].astype(jnp.float32)
+        delta.append(jnp.sum(both.T, 0, keepdims=True))
+
+    def body(kb, carry):
+        k0 = pl.multiple_of(kb * BK, BK)
+        key = lax.broadcasted_iota(jnp.int32, (BK, BQ), 0) + k0
+        mask = (key >= start) & (key < end)
+        q = [qkv_ref[pl.ds(q0, BQ), h * HD : (h + 1) * HD] for h in span]
+        do = [do_ref[pl.ds(q0, BQ), h * HD : (h + 1) * HD] for h in span]
+        s = [
+            dot_nt(qkv_ref[pl.ds(k0, BK), local + h * HD : local + (h + 1) * HD], q[h])
+            for h in span
+        ]
+        dp = [
+            dot_nt(qkv_ref[pl.ds(k0, BK), 2 * local + h * HD : 2 * local + (h + 1) * HD], do[h])
+            for h in span
+        ]
+        p = [
+            jnp.exp(jnp.where(mask, s[h], NEG) - lse_ref[h : h + 1, pl.ds(q0, BQ)]) for h in span
+        ]
+        ds = [(p[h] * (dp[h] - delta[h])).astype(jnp.bfloat16) for h in span]
+        pb = [p[h].astype(jnp.bfloat16) for h in span]
+        for h in span:
+            dv_s[h, pl.ds(k0, BK), :] += dot_nn(pb[h], do[h])
+        for h in span:
+            dk_s[h, pl.ds(k0, BK), :] += dot_nn(ds[h], q[h])
+        for h in span:
+            dq_s[h] += dot_nn(kt_ref[h * HD : (h + 1) * HD, pl.ds(k0, BK)], ds[h])
+        return carry
+
+    lax.fori_loop(klo[i], khi[i], body, 0)
+    for h in span:
+        dq = dq_s[h].T * 0.125
+        d_ref[pl.ds(q0, BQ), h * HD : (h + 1) * HD] = dq.astype(jnp.bfloat16)
+        dbq_ref[h : h + 1, :] += jnp.sum(dq, 0, keepdims=True)
+
+    @pl.when(i == n - 1)
+    def _():
+        for h in span:
+
+            def finish(j, carry):
+                r = pl.ds(pl.multiple_of(j * BK, BK), BK)
+                dk = dk_s[h, r, :]
+                dv = dv_s[h, r, :]
+                d_ref[r, local + h * HD : local + (h + 1) * HD] = dk.astype(jnp.bfloat16)
+                d_ref[r, 2 * local + h * HD : 2 * local + (h + 1) * HD] = dv.astype(jnp.bfloat16)
+                return carry + jnp.sum(dv, 0, keepdims=True)
+
+            dbv_ref[h : h + 1, :] = lax.fori_loop(0, n, finish, jnp.zeros((1, HD), jnp.float32))
+
+
+def attend_back(qkv, kt, do, ctx, lse, seg, klo, khi, heads):
+    rows = qkv.shape[0]
+    local = heads * HD
+
+    def const(shape):
+        return pl.BlockSpec(shape, lambda i, *_: (0, 0), pipeline_mode=pl.Buffered(1))
+
+    tall = pltpu.VMEM((heads, rows, HD), jnp.float32)
+    return pl.pallas_call(
+        functools.partial(attend_back_kernel, heads),
+        out_shape=(
+            jax.ShapeDtypeStruct((rows, 3 * local), jnp.bfloat16),
+            jax.ShapeDtypeStruct((8, HD), jnp.float32),
+            jax.ShapeDtypeStruct((8, HD), jnp.float32),
+        ),
+        grid_spec=pltpu.PrefetchScalarGridSpec(
+            num_scalar_prefetch=2,
+            grid=(rows // BQ,),
+            in_specs=[whole(qkv), whole(kt), whole(do), whole(ctx), whole(lse), whole(seg)],
+            out_specs=[const((rows, 3 * local)), const((8, HD)), const((8, HD))],
+            scratch_shapes=[tall, tall, pltpu.VMEM((heads, HD, BQ), jnp.float32)],
+        ),
+        compiler_params=pltpu.CompilerParams(vmem_limit_bytes=60 << 20),
+        name="attend_back",
+    )(klo, khi, qkv, kt, do, ctx, lse, seg)
+
+
+def packed_step(size, cids, offset, length, offsets, lengths, args):
+    (
+        tokens, _, _, w_qkv, bias_q, bias_v, w_out, bias_out, w_up, bias_up, w_down, bias_down,
+        gain1, shift1, gain2, shift2, grad_out,
+    ) = args
+    f32, bf16 = jnp.float32, jnp.bfloat16
+    cap, width = tokens.shape
+    local = w_qkv.shape[2]
+    heads = local // HD
+    rows = 32 * size
+    mine = 4 * size
+    dp = lax.axis_index("dp")
+    t = lax.axis_index("tensor")
+    pack_id, gather_id, share_id, last_id = cids
+
+    def own(value, count=mine, at=None):
+        first = dp * mine if at is None else at
+        return lax.dynamic_slice_in_dim(value, first, count, 0)
+
+    at_block = (dp * 4 + t) * size
+    info = jnp.stack([offset, length])
+    x_parts, up_parts = take_pieces(tokens, grad_out, info, size)
+    x_all = pack_gather(x_parts, pack_id)
+    up_all = pack_gather(up_parts, pack_id)
+
+    index = jnp.arange(rows, dtype=jnp.int32)
+    inside = (index[None, :] >= offsets[:, None]) & (index[None, :] < (offsets + lengths)[:, None])
+    start = jnp.sum(jnp.where(inside, offsets[:, None], 0), 0)
+    end = jnp.sum(jnp.where(inside, (offsets + lengths)[:, None], 0), 0)
+    seg = jnp.concatenate([start[None], end[None], jnp.zeros((6, rows), jnp.int32)], 0)
+    taken = end > 0
+    first_key = jnp.min(jnp.where(taken, start, rows).reshape(-1, BQ), 1)
+    last_key = jnp.max(end.reshape(-1, BQ), 1)
+    klo = jnp.where(last_key > 0, first_key // BK, 0)
+    khi = (last_key + BK - 1) // BK
+
+    _, _, pre1 = layer_norm(x_all.astype(f32), gain1, shift1)
+    act1 = pre1.astype(bf16)
+    joined = w_qkv.reshape(width, 3 * local)
+    bias = jnp.concatenate([bias_q, jnp.zeros_like(bias_q), bias_v])
+    scale = jnp.concatenate([jnp.full((local,), HD**-0.5, bf16), jnp.ones((2 * local,), bf16)])
+    qkv = (jnp.dot(act1, joined, preferred_element_type=f32) + bias).astype(bf16) * scale
+    context, lse = attend(qkv, qkv[:, 2 * local :].T, seg, klo, khi, heads)
+    part = jnp.dot(own(context), w_out, preferred_element_type=f32).astype(bf16)
+    attended = share4(part, share_id)
+    source = own(x_all, size, at_block).astype(f32)
+    middle = source + attended + bias_out
+    normed2, rstd2, pre2 = layer_norm(middle, gain2, shift2)
+    (act2,) = gather32([pre2.astype(bf16)], [cap], gather_id)
+    act2 = act2[:rows]
+
+    pre = jnp.dot(act2, w_up, preferred_element_type=f32) + bias_up
+    hidden_f, slope = gelu_pair(pre)
+    hidden = hidden_f.astype(bf16)
+    d_pre = contract_last(up_all, w_down) * slope
+    g_up_bias = jnp.sum(d_pre, 0)
+    d_pre_b = d_pre.astype(bf16)
+    d_act2 = share4(contract_last(own(d_pre_b), w_up).astype(bf16), share_id)
+    upstream = own(up_all, size, at_block).astype(f32)
+    d_middle = upstream + layer_norm_back(d_act2, normed2, rstd2, gain2)
+    (d_middle_b,) = gather32([d_middle.astype(bf16)], [cap], gather_id)
+    d_middle_b = d_middle_b[:rows]
+    g_down = contract_first(hidden, up_all)
+    g_up = contract_first(act2, d_pre_b)
+    g_down_bias = jnp.sum(up_all.astype(f32), 0)
+    branch = share4(
+        jnp.dot(own(hidden), w_down, preferred_element_type=f32).astype(bf16), share_id
+    )
+    (mixed_all,) = gather32([(middle + branch + bias_down).astype(bf16)], [cap], gather_id)
+
+    g_out_bias = jnp.sum(d_middle_b.astype(f32), 0)
+    g_out = contract_first(context, d_middle_b)
+    d_context = contract_last(d_middle_b, w_out).astype(bf16)
+    d_qkv, dbq, dbv = attend_back(
+        qkv, qkv[:, local : 2 * local].T, d_context, context, lse, seg, klo, khi, heads
+    )
+    g_bias_q = dbq[:heads].reshape(local)
+    g_bias_v = dbv[:heads].reshape(local)
+    g_qkv = contract_first(act1, d_qkv).reshape(width, 3, local)
+    d_act1 = share4(contract_last(own(d_qkv), joined).astype(bf16), share_id)
+    normed1, rstd1, _ = layer_norm(source, gain1, shift1)
+    d_tokens = d_middle + layer_norm_back(d_act1, normed1, rstd1, gain1)
+    vectors = jnp.stack(
+        [
+            jnp.sum(d_act1 * normed1, 0),
+            jnp.sum(d_act1, 0),
+            jnp.sum(d_act2 * normed2, 0),
+            jnp.sum(d_act2, 0),
+        ]
+        + [jnp.zeros((width,), f32)] * 4
+    )
+    d_tokens_all, vectors_all = gather32([d_tokens.astype(bf16), vectors], [cap, 0], last_id)
+    sums = jnp.sum(vectors_all.reshape(32, 8, width), 0)
+    valid = (jnp.arange(cap, dtype=jnp.int32) < length)[:, None]
+
+    def slot(value):
+        return jnp.where(valid, own(value, cap, offset), jnp.zeros((), value.dtype))
+
+    return (
+        slot(mixed_all),
+        slot(d_tokens_all).astype(f32),
+        g_qkv,
+        g_bias_q,
+        g_bias_v,
+        g_out,
+        g_out_bias,
+        g_up,
+        g_up_bias,
+        g_down,
+        g_down_bias,
+        sums[0],
+        sums[1],
+        sums[2],
+        sums[3],
+    )
+
+
+def packed(*args):
+    clip_len, slot_clip = args[1], args[2]
+    clips = clip_len.shape[0]
+
+    def padded(value):
+        return (value + 15) // 16 * 16
+
+    need = jnp.sum(padded(clip_len))
+    table = gather_table(slot_clip[0], 0)
+    match = table[:, None] == jnp.arange(clips, dtype=jnp.int32)[None, :]
+    lengths = jnp.sum(jnp.where(match, clip_len[None, :], 0), 1)
+    offsets = jnp.cumsum(padded(lengths)) - padded(lengths)
+    dp = lax.axis_index("dp")
+    length = lengths[dp]
+    offset = offsets[dp]
+    branches = [
+        functools.partial(packed_step, size, [1 + 4 * n + i for i in range(4)])
+        for n, size in enumerate(BLOCKS)
+    ]
+    pick = sum((need > 32 * size).astype(jnp.int32) for size in BLOCKS)
+
+    def fallback(offset, length, offsets, lengths, args):
+        return plain(*args)
+
+    return lax.switch(pick, branches + [fallback], offset, length, offsets, lengths, args)
+
+
 def solution(mesh):
     placed = (
         P("dp", None),
@@ -260,8 +1103,9 @@
         P(),
         P("dp", None),
     )
+    fits = mesh.shape["dp"] == 8 and mesh.shape["tensor"] == 4
     return jax.shard_map(
-        shards,
+        packed if fits else plain,
         mesh=mesh,
         in_specs=placed,
         out_specs=(

time: 867 us -> 778 us (0.90)
  Pallas kernels: 0 us -> 563 us
  waiting for transfers between devices: 520 us -> 0 us
  other arithmetic: 97 us -> 31.4 us
  matrix products: 182 us -> 120 us
  blocking collectives: 39.1 us -> 0 us
  local copies, waits for them, and re-layouts: 7.6 us -> 28.3 us
  loops' own time: 0 us -> 10.6 us
    pallas_call x0 -> x14, Pallas kernels: none -> 563 us  [the longest x4 195 us: gather32(): pl.pallas_call(gather_kernel, out_shape=[jax.ShapeDtypeStruct((32 * a.sha...]
    psum x4 -> x0, waiting for transfers between devices: 520 us -> none  [the longest x1 248 us: shards(): lax.psum(g_qkv.astype(jnp.bfloat16), 'dp').astype(jnp.float32)]
    dot_general x10 -> x4, matrix products: 132 us -> 32.1 us  [the longest x1 16.9 us: packed_step(): pre = jnp.dot(act2, w_up, preferred_element_type=f32) + bias_up]
    psum x1 -> x0, blocking collectives: 39.1 us -> none  [shards(): lax.psum(g_bias_q.astype(jnp.bfloat16), 'dp').astype(jnp.float32)]
    reduce_sum x8, other arithmetic: 47 us -> 10.7 us  [the longest x1 5.1 us: packed_step(): g_out_bias = jnp.sum(d_middle_b.astype(f32), 0)]
    dot_general x4, matrix products: 26.2 us -> 54.3 us  [contract_first(): lax.dot_general(left, right, (((0,), (0,)), ((), ())), preferred_element_...]
    select_n x1, other arithmetic: 15.5 us -> 0.01 us  [packed_step(): khi = (last_key + BK - 1) // BK]
    another operation x0 -> x1, loops' own time: none -> 10.6 us  [packed(): lax.switch(pick, branches + [fallback], offset, length, offsets, lengths,...]
  transfers between devices with their start and end apart: 4 -> 0, of which waited for: 4 -> 0; matrix products, arithmetic and copies ran while one was open for 8% -> 0% of each run, Pallas kernels for 0% -> 0%
where the time goes in v1:
time: 778 us; the launch traced here: 769 us
  Pallas kernels  563 us (72%)
  matrix products  120 us (15%)
  other arithmetic  31.4 us (4%)
  local copies, waits for them, and re-layouts  28.3 us (4%)
  between operations  15.6 us (2%)
  loops' own time  10.6 us (1%)
    pallas_call x4, Pallas kernels, gather32(): pl.pallas_call(gather_kernel, out_shape=[jax.ShapeDtypeStruct((32 * a.sha...  195 us
    pallas_call x2, Pallas kernels, pack_gather(): pl.pallas_call(pack_kernel, out_shape=jax.ShapeDtypeStruct((32 * size, wi...  148 us
    pallas_call x1, Pallas kernels, attend_back(): pl.pallas_call(functools.partial(attend_back_kernel, heads), out_shape=(j...  96.9 us
    pallas_call x1, Pallas kernels, attend(): pl.pallas_call(functools.partial(attend_kernel, heads), out_shape=(jax.Sh...  55.9 us
    dot_general x4, matrix products, contract_first(): lax.dot_general(left, right, (((0,), (0,)), ((), ())), preferred_element_...  54.3 us
    pallas_call x4, Pallas kernels, share4(): pl.pallas_call(share_kernel, out_shape=jax.ShapeDtypeStruct((size, width)...  52.6 us
    dot_general x4, matrix products, contract_last(): lax.dot_general(left, right, (((1,), (1,)), ((), ())), preferred_element_...  33.4 us
    dot_general x1, matrix products, packed_step(): pre = jnp.dot(act2, w_up, preferred_element_type=f32) + bias_up  16.9 us

profile of v1, /device:TPU:0, one launch (start us, length us, event | category | flops | bytes accessed | tf_op | source)
XLA Modules:
  0.0 768.8 jit_solution(1338975742355795111)
XLA Ops:
  8.4 9.7 %table.1 = s32[8,8,128]{2,1,0:T(8,128)} custom-call(s32[8,128]{1,0:T(8,128)} %broadcast_in_dim.186.x_ref), custom_call_target="tpu_custom_call" | custom-call | tf_op jit(solution)/shard_map/table/pallas_call | solution.py:479
  18.2 1.0 slice_reduce_fusion.4
  19.2 0.8 select_reduce_fusion.3
  20.2 1.3 multiply_reduce_fusion.7
  22.2 739.5 %conditional.1 = (bf16[1536,1280]{1,0:T(8,128)(2,1)}, f32[1536,1280]{1,0:T(8,128)}, f32[1280,3,320]{0,2,1:T(8,128)}, f32[320]{0:T(512)}, f32[320]{0:T(512)}, /*i...) conditional(s32[]{:T(128)} %clamp.3, (s32[]{:T(128)}, ...), branch_computations={%region_3.26_spmd, %region_26.65_spmd} | conditional | flops 64355631104 | bytes 1081512320 | solution.py:1083
  23.4 1.4 pad_add_fusion.info_ref
  24.8 4.3 pieces.1
  29.1 1.3 copy-done.5
  30.4 75.4 %pack_gather.2 = bf16[3072,1280]{1,0:T(8,128)(2,1)S(1)} custom-call(bf16[8,96,1280]{2,1,0:T(8,128)(2,1)S(1)} %get-tuple-element.193.p_ref), custom_call_target="tpu_custom_call" | custom-call | tf_op jit(solution)/shard_map/cond/branch_0_fun/pack_gather/pallas_call | solution.py:685
  105.9 1.1 convert_reduce_fusion.1
  107.0 2.2 fusion.61
  109.5 10.9 %fusion.78 = bf16[3072,960]{0,1:T(8,128)(2,1)} fusion(f32[960]{0:T(1024)S(1)} %pad_maximum_fusion.3, bf16[1280,960]{0,1:T(8,128)(2,1)S(1)} %bitcast.125, bf16[960]{0:T(1024)(128)(2,1)S(1)} %copy-done.66, bf16[3072,1280]{1,0:T(8,128)(2,1)S(1)} %pack_gather.2, f32[1280]{0:T(1024)S(1)} %copy-done.60, f32[1280]{0:T(1024)S(1)} %copy-done.38, ...), kind=kOutput, calls=%fused_computation.124 | convolution fusion | flops 7582187520 | bytes 16260736 | tf_op jit(solution)/shard_map/cond/branch_0_fun/dot_general | solution.py:983
  120.4 8.5 %copy.88.qkv_ref = bf16[3072,960]{1,0:T(8,128)(2,1)} copy(bf16[3072,960]{0,1:T(8,128)(2,1)} %fusion.78) | data formatting | bytes 11796480 | tf_op jit(solution)/shard_map/cond/branch_0_fun/mul | solution.py:983
  129.0 3.7 slice_bitcast_fusion
  133.2 2.8 copy-done.1
  136.0 55.9 %attend.1 = (bf16[3072,320]{1,0:T(8,128)(2,1)S(1)}, f32[8,3072]{1,0:T(8,128)S(1)}) custom-call(s32[12]{0:T(128)S(1)} %get-tuple-element.384.klo, s32[12]{0:T(128)S(1)} %get-tuple-element.383.khi, bf16[3072,960]{1,0:T(8,128)(2,1)S(1)} %copy-done.1, bf16[320,3072]{1,0:T(8,128)(2,1)S(1)} %get-tuple-element.379.vt_ref, s32[8,3072]{1,0:T(8,128)S(1)} %add_add_fusion.seg_ref), custom_call_target="tpu_custom_call" | custom-call | tf_op jit(solution)/shard_map/cond/branch_0_fun/attend/pallas_call | solution.py:821
  191.9 1.4 copy-done.3
  193.9 1.6 convolution_convert_fusion.11
  195.6 13.2 %share4.4 = f32[96,1280]{1,0:T(8,128)S(1)} custom-call(bf16[4,96,1280]{2,1,0:T(8,128)(2,1)S(1)} %bitcast.94), custom_call_target="tpu_custom_call" | custom-call | tf_op jit(solution)/shard_map/cond/branch_0_fun/share4/pallas_call | solution.py:744
  208.8 1.1 convert_reduce_fusion.4
  209.9 1.2 fusion.111
  211.3 0.8 add_convert_fusion.5.refs_0_
  212.2 42.2 %gather32.4 = bf16[4608,1280]{1,0:T(8,128)(2,1)} custom-call(bf16[96,1280]{1,0:T(8,128)(2,1)} %add_convert_fusion.5.refs_0_), custom_call_target="tpu_custom_call" | custom-call | tf_op jit(solution)/shard_map/cond/branch_0_fun/gather32/pallas_call | solution.py:440
  254.5 16.9 %multiply_convert_fusion.2 = (bf16[3072,1280]{1,0:T(8,128)(2,1)}, f32[3072,1280]{1,0:T(8,128)}) fusion(f32[1280]{0:T(1024)S(1)} %copy-done.63, bf16[1280,1280]{1,0:T(8,128)(2,1)} %get-tuple-element.204, bf16[4608,1280]{1,0:T(8,128)(2,1)} %gather32.4), kind=kOutput, calls=%fused_computation.113 | convolution fusion | flops 10089922560 | bytes 34739200 | tf_op jit(solution)/shard_map/cond/branch_0_fun/dot_general | solution.py:993
  271.4 72.8 %pack_gather.3 = bf16[3072,1280]{1,0:T(8,128)(2,1)S(1)} custom-call(bf16[8,96,1280]{2,1,0:T(8,128)(2,1)S(1)} %copy-done.6), custom_call_target="tpu_custom_call" | custom-call | tf_op jit(solution)/shard_map/cond/branch_0_fun/pack_gather/pallas_call | solution.py:685
  344.2 21.2 %fusion.118 = (f32[1280]{0:T(1024)}, bf16[3072,1280]{1,0:T(8,128)(2,1)}) fusion(f32[3072,1280]{1,0:T(8,128)} %get-tuple-element.387, f32[1280]{0:T(1024)S(1)} %copy-done.63, bf16[3072,1280]{1,0:T(8,128)(2,1)S(1)} %pack_gather.3, bf16[1280,1280]{1,0:T(8,128)(2,1)S(1)} %copy-done.55), kind=kOutput, calls=%fused_computation.231 | convolution fusion | flops 10113514496 | bytes 34744320 | tf_op jit(solution)/shard_map/cond/branch_0_fun/dot_general | solution.py:47
  365.4 2.7 convolution_convert_fusion.12
  368.1 13.2 %share4.6 = f32[96,1280]{1,0:T(8,128)S(1)} custom-call(bf16[4,96,1280]{2,1,0:T(8,128)(2,1)S(1)} %bitcast.96), custom_call_target="tpu_custom_call" | custom-call | tf_op jit(solution)/shard_map/cond/branch_0_fun/share4/pallas_call | solution.py:744
  381.6 2.6 convolution_convert_fusion.13
  384.2 13.1 %share4.5 = f32[96,1280]{1,0:T(8,128)S(1)} custom-call(bf16[4,96,1280]{2,1,0:T(8,128)(2,1)S(1)} %bitcast.97), custom_call_target="tpu_custom_call" | custom-call | tf_op jit(solution)/shard_map/cond/branch_0_fun/share4/pallas_call | solution.py:744
  397.4 1.1 fusion.110
  398.5 44.4 %gather32.6 = bf16[4608,1280]{1,0:T(8,128)(2,1)} custom-call(bf16[96,1280]{1,0:T(8,128)(2,1)} %get-tuple-element.350.refs_0_), custom_call_target="tpu_custom_call" | custom-call | tf_op jit(solution)/shard_map/cond/branch_0_fun/gather32/pallas_call | solution.py:440
  442.9 7.2 fusion.79
  450.2 4.1 copy.90.do_ref
  454.2 96.9 %attend_back.1 = (bf16[3072,960]{1,0:T(8,128)(2,1)}, f32[8,64]{1,0:T(8,128)}, f32[8,64]{1,0:T(8,128)}) custom-call(s32[12]{0:T(128)} %copy-done.10, s32[12]{0:T(128)} %copy-done.9, bf16[3072,960]{1,0:T(8,128)(2,1)} %copy.88.qkv_ref, bf16[320,3072]{1,0:T(8,128)(2,1)} %get-tuple-element.378.kt_ref, bf16[3072,320]{1,0:T(8,128)(2,1)} %copy.90.do_ref, ...), custom_call_target="tpu_custom_call" | custom-call | tf_op jit(solution)/shard_map/cond/branch_0_fun/attend_back/pallas_call | solution.py:923
  551.2 16.3 %fusion.104 = f32[1280,960]{0,1:T(8,128)} fusion(bf16[3072,960]{1,0:T(8,128)(2,1)} %get-tuple-element.210, bf16[3072,1280]{1,0:T(8,128)(2,1)} %copy-done, f32[1280]{0:T(1024)S(1)} %copy-done.60, f32[1280]{0:T(1024)S(1)} %copy-done.38, f32[3072]{0:T(1024)S(1)} %add_rsqrt_fusion.2, f32[3072]{0:T(1024)S(1)} %broadcast_multiply_fusion.6), kind=kOutput, calls=%fused_computation.206 | convolution fusion | flops 7573340160 | bytes 18712576 | tf_op jit(solution)/shard_map/cond/branch_0_fun/dot_general | solution.py:41
  567.5 2.3 convolution_convert_fusion.10
  569.8 13.2 %share4.7 = f32[96,1280]{1,0:T(8,128)S(1)} custom-call(bf16[4,96,1280]{2,1,0:T(8,128)(2,1)S(1)} %bitcast.95), custom_call_target="tpu_custom_call" | custom-call | tf_op jit(solution)/shard_map/cond/branch_0_fun/share4/pallas_call | solution.py:744
  583.0 1.3 fusion.95
  585.0 1.9 fusion.94.refs_0_
  586.9 65.1 %gather32.7 = (bf16[4608,1280]{1,0:T(8,128)(2,1)}, f32[256,1280]{1,0:T(8,128)}) custom-call(bf16[96,1280]{1,0:T(8,128)(2,1)} %fusion.94.refs_0_, f32[8,1280]{1,0:T(8,128)} %stack.17.refs_1_), custom_call_target="tpu_custom_call" | custom-call | tf_op jit(solution)/shard_map/cond/branch_0_fun/gather32/pallas_call | solution.py:440
  652.0 43.6 %gather32.5 = bf16[4608,1280]{1,0:T(8,128)(2,1)} custom-call(bf16[96,1280]{1,0:T(8,128)(2,1)} %get-tuple-element.380.refs_0_), custom_call_target="tpu_custom_call" | custom-call | tf_op jit(solution)/shard_map/cond/branch_0_fun/gather32/pallas_call | solution.py:440
  698.2 8.4 %select_convert_fusion.1 = (f32[1536,1280]{1,0:T(8,128)}, bf16[1536,1280]{1,0:T(8,128)(2,1)}) fusion(bf16[4608,1280]{1,0:T(8,128)(2,1)} %get-tuple-element.211, s32[]{:T(128)S(6)} %select_n.86, pred[1536]{0:T(1024)(128)(4,1)S(1)} %iota_compare_fusion.3, bf16[4608,1280]{1,0:T(8,128)(2,1)} %gather32.5), kind=kLoop, calls=%fused_computation.126 | loop fusion | flops 5898240 | bytes 19662340 | tf_op jit(solution)/shard_map/cond/branch_0_fun/convert_element_type | solution.py:1042
  706.6 17.0 %fusion.70 = f32[1280,1280]{1,0:T(8,128)} fusion(bf16[3072,1280]{1,0:T(8,128)(2,1)} %get-tuple-element.376, bf16[4608,1280]{1,0:T(8,128)(2,1)} %gather32.4), kind=kOutput, calls=%fused_computation.116 | convolution fusion | flops 10066329600 | bytes 22282240 | tf_op jit(solution)/shard_map/cond/branch_0_fun/dot_general | solution.py:41
  723.6 3.9 fusion.74
  729.6 5.1 convert_reduce_fusion.3
  734.7 17.2 %fusion.119 = f32[1280,1280]{1,0:T(8,128)} fusion(bf16[3072,1280]{1,0:T(8,128)(2,1)} %get-tuple-element.386, bf16[3072,1280]{1,0:T(8,128)(2,1)} %copy-done.2), kind=kOutput, calls=%fused_computation.232 | convolution fusion | flops 10066329600 | bytes 22282240 | tf_op jit(solution)/shard_map/cond/branch_0_fun/dot_general | solution.py:41
  751.9 1.7 convert_reduce_fusion.2
  (109 shorter events, 7.4 us)
Async XLA Ops:
  29.1 1.3 copy-start.5
  105.8 3.6 copy-start
  105.8 3.4 copy-start.45
  105.8 3.4 copy-start.47
  105.8 3.6 copy-start.38
  105.8 3.6 copy-start.57
  105.9 3.6 copy-start.60
  105.9 3.6 copy-start.66
  129.0 65.0 %copy-start.25 = (bf16[320,1280]{1,0:T(8,128)(2,1)S(1)}, bf16[320,1280]{1,0:T(8,128)(2,1)}, u32[]{:S(2)}) copy-start(bf16[320,1280]{1,0:T(8,128)(2,1)} %get-tuple-element.200) | copy-start | bytes 2457604 | tf_op jit(solution)/shard_map/cond
  132.7 77.2 %copy-start.32 = (f32[1280]{0:T(1024)S(1)}, f32[1280]{0:T(1024)}, u32[]{:S(2)}) copy-start(f32[1280]{0:T(1024)} %get-tuple-element.201) | copy-start | bytes 15364 | tf_op jit(solution)/shard_map/cond
  132.7 78.6 %copy-start.34 = (f32[1280]{0:T(1024)S(1)}, f32[1280]{0:T(1024)}, u32[]{:S(2)}) copy-start(f32[1280]{0:T(1024)} %get-tuple-element.202) | copy-start | bytes 15364 | tf_op jit(solution)/shard_map/cond
  132.7 78.6 %copy-start.49 = (f32[1280]{0:T(1024)S(1)}, f32[1280]{0:T(1024)}, u32[]{:S(2)}) copy-start(f32[1280]{0:T(1024)} %get-tuple-element.203) | copy-start | bytes 15364 | tf_op jit(solution)/shard_map/cond
  133.0 121.4 %copy-start.9 = (s32[12]{0:T(128)}, s32[12]{0:T(128)S(1)}, u32[]{:S(2)}) copy-start(s32[12]{0:T(128)S(1)} %get-tuple-element.383.khi) | copy-start | bytes 148 | tf_op jit(solution)/shard_map/cond
  133.0 121.4 %copy-start.10 = (s32[12]{0:T(128)}, s32[12]{0:T(128)S(1)}, u32[]{:S(2)}) copy-start(s32[12]{0:T(128)S(1)} %get-tuple-element.384.klo) | copy-start | bytes 148 | tf_op jit(solution)/shard_map/cond
  133.2 2.8 copy-start.1
  136.0 118.5 %copy-start.7 = (s32[8,3072]{1,0:T(8,128)}, s32[8,3072]{1,0:T(8,128)S(1)}, u32[]{:S(2)}) copy-start(s32[8,3072]{1,0:T(8,128)S(1)} %add_add_fusion.seg_ref) | copy-start | bytes 294916 | tf_op jit(solution)/shard_map/cond
  191.8 1.4 copy-start.3
  193.3 0.6 copy-start.8
  195.6 58.9 %copy-start.63 = (f32[1280]{0:T(1024)S(1)}, f32[1280]{0:T(1024)}, u32[]{:S(2)}) copy-start(f32[1280]{0:T(1024)} %get-tuple-element.205) | copy-start | bytes 15364 | tf_op jit(solution)/shard_map/cond
  254.5 16.9 %copy-start.6 = (bf16[8,96,1280]{2,1,0:T(8,128)(2,1)S(1)}, bf16[8,96,1280]{2,1,0:T(8,128)(2,1)}, u32[]{:S(2)}) copy-start(bf16[8,96,1280]{2,1,0:T(8,128)(2,1)} %copy-done.5) | copy-start | bytes 5898244 | tf_op jit(solution)/shard_map/cond
  271.4 72.8 %copy-start.55 = (bf16[1280,1280]{1,0:T(8,128)(2,1)S(1)}, bf16[1280,1280]{1,0:T(8,128)(2,1)}, u32[]{:S(2)}) copy-start(bf16[1280,1280]{1,0:T(8,128)(2,1)} %get-tuple-element.206) | copy-start | bytes 9830404 | tf_op jit(solution)/shard_map/cond
  344.1 53.2 %copy-start.2 = (bf16[3072,1280]{1,0:T(8,128)(2,1)}, bf16[3072,1280]{1,0:T(8,128)(2,1)S(1)}, u32[]{:S(2)}) copy-start(bf16[3072,1280]{1,0:T(8,128)(2,1)S(1)} %pack_gather.3) | copy-start | bytes 23592964 | tf_op jit(solution)/shard_map/cond
  344.2 21.2 %copy-start.53 = (bf16[1280,1280]{1,0:T(8,128)(2,1)S(1)}, bf16[1280,1280]{1,0:T(8,128)(2,1)}, u32[]{:S(2)}) copy-start(bf16[1280,1280]{1,0:T(8,128)(2,1)} %get-tuple-element.204) | copy-start | bytes 9830404 | tf_op jit(solution)/shard_map/cond
  368.1 29.3 %copy-start.43 = (f32[1280]{0:T(1024)S(1)}, f32[1280]{0:T(1024)}, u32[]{:S(2)}) copy-start(f32[1280]{0:T(1024)} %get-tuple-element.207) | copy-start | bytes 15364 | tf_op jit(solution)/shard_map/cond
  551.2 16.3 %copy-start.58 = (bf16[1280,3,320]{0,2,1:T(8,128)(2,1)S(1)}, bf16[1280,3,320]{0,2,1:T(8,128)(2,1)}, u32[]{:S(2)}) copy-start(bf16[1280,3,320]{0,2,1:T(8,128)(2,1)} %get-tuple-element.196) | copy-start | bytes 7372804 | tf_op jit(solution)/shard_map/cond
  698.2 25.4 %slice-start.4 = ((s8[11796480]{0:T(1024)(128)(4,1)}), s8[4194304]{0:T(1024)(128)(4,1)S(1)}, s32[]{:S(2)}) async-start(s8[11796480]{0:T(1024)(128)(4,1)} %bitcast.100), calls=%async_computation.8 | async-start | bytes 8388608 | tf_op jit(solution)/shard_map/cond
  706.6 17.0 %copy-start.4 = (bf16[3072,320]{1,0:T(8,128)(2,1)S(1)}, bf16[3072,320]{1,0:T(8,128)(2,1)}, u32[]{:S(2)}) copy-start(bf16[3072,320]{1,0:T(8,128)(2,1)} %copy-done.3) | copy-start | bytes 5898244 | tf_op jit(solution)/shard_map/cond
  706.6 17.0 %slice-start.5 = ((s8[11796480]{0:T(1024)(128)(4,1)}), s8[4194304]{0:T(1024)(128)(4,1)S(1)}, s32[]{:S(2)}) async-start(s8[11796480]{0:T(1024)(128)(4,1)} %bitcast.100), calls=%async_computation.9 | async-start | bytes 8388608 | tf_op jit(solution)/shard_map/cond
  706.6 17.0 %slice-start.6 = ((s8[11796480]{0:T(1024)(128)(4,1)}), s8[3407872]{0:T(1024)(128)(4,1)S(1)}, s32[]{:S(2)}) async-start(s8[11796480]{0:T(1024)(128)(4,1)} %bitcast.100), calls=%async_computation.10 | async-start | bytes 6815744 | tf_op jit(solution)/shard_map/cond
  723.6 4.0 copy-start.29
  723.6 4.7 copy-start.52
  723.6 5.3 copy-start.51
  729.6 22.3 %slice-start = ((s8[7864320]{0:T(1024)(128)(4,1)}), s8[4194304]{0:T(1024)(128)(4,1)S(1)}, s32[]{:S(2)}) async-start(s8[7864320]{0:T(1024)(128)(4,1)} %bitcast.92), calls=%async_computation.4 | async-start | bytes 8388608 | tf_op jit(solution)/shard_map/cond
  734.7 17.2 %slice-start.1 = ((s8[7864320]{0:T(1024)(128)(4,1)}), s8[3670016]{0:T(1024)(128)(4,1)S(1)}, s32[]{:S(2)}) async-start(s8[7864320]{0:T(1024)(128)(4,1)} %bitcast.92), calls=%async_computation.5 | async-start | bytes 7340032 | tf_op jit(solution)/shard_map/cond

commit v2 on v1

--- a/solution.py
+++ b/solution.py
@@ -254,6 +254,10 @@
 BK = 256
 
 
+def cost(us):
+    return pl.CostEstimate(flops=int(us * 1e9), bytes_accessed=int(us * 3e6), transcendentals=0)
+
+
 def coords():
     dp = lax.axis_index("dp")
     t = lax.axis_index("tensor")
@@ -296,62 +300,74 @@
 GATHER_SEMS = [DMA, DMA((4,)), DMA((4,)), DMA((4,)), DMA((8,)), DMA((16,)), DMA((32,))]
 
 
-def gather_steps(x_ref, o_ref, local_sem, right_sem, left_sem, u_sem, v_sem, core_sem, recv_sem):
+def gather_steps(x_refs, o_refs, sems, work=None, ahead=None):
     z, y, x, c = coords()
-    size = x_ref.shape[0]
+    n = len(GATHER_SEMS)
+    arrays = [(a, o) + tuple(sems[n * i : n * i + n]) for i, (a, o) in enumerate(zip(x_refs, o_refs))]
 
     def block(z, y, x, c):
         return (z * 2 + y) * 4 + x * 2 + c
 
-    def rows(b):
-        return o_ref.at[pl.ds(pl.multiple_of(b * size, size), size)]
-
     ux, uy = x + (1 - c) * (1 - 2 * x), y + c * (1 - 2 * y)
     vx, vy = x + c * (1 - 2 * x), y + (1 - c) * (1 - 2 * y)
-
-    def copy(b, src, sem, peer):
+    own = block(z, y, x, c)
+    core = device(z, y, x, 1 - c)
+
+    def rows(array, b):
+        size = array[0].shape[0]
+        return array[1].at[pl.ds(pl.multiple_of(b * size, size), size)]
+
+    def copy(array, b, kind, i, peer):
         return pltpu.make_async_remote_copy(
-            src_ref=src,
-            dst_ref=rows(b),
-            send_sem=sem,
-            recv_sem=recv_sem.at[b],
+            src_ref=rows(array, b),
+            dst_ref=rows(array, b),
+            send_sem=array[kind].at[i],
+            recv_sem=array[8].at[b],
             device_id=peer,
             device_id_type=MESH,
         )
 
-    def send_right(b, src, i):
-        copy(b, src, right_sem.at[i], device(z + 1, y, x, c)).start()
-
-    def send_left(b, src, i):
-        copy(b, src, left_sem.at[i], device(z - 1, y, x, c)).start()
-
-    def send_u(b, src, i):
-        copy(b, src, u_sem.at[i], device(z, uy, ux, c)).start()
-
-    def send_v(b, src, i):
-        copy(b, src, v_sem.at[i], device(z, vy, vx, c)).start()
-
-    def send_core(b, src, i):
-        copy(b, src, core_sem.at[i], device(z, y, x, 1 - c)).start()
+    def send(b, kind, i, peer, first=False):
+        for array in arrays:
+            if first:
+                pltpu.make_async_remote_copy(
+                    src_ref=array[0],
+                    dst_ref=rows(array, b),
+                    send_sem=array[kind].at[i],
+                    recv_sem=array[8].at[b],
+                    device_id=peer,
+                    device_id_type=MESH,
+                ).start()
+            else:
+                copy(array, b, kind, i, peer).start()
 
     def arrived(b):
-        copy(b, x_ref, core_sem.at[0], device(z, y, x, 1 - c)).wait_recv()
-
-    own = block(z, y, x, c)
-    local = pltpu.make_async_copy(x_ref, rows(own), local_sem)
-    local.start()
+        for array in arrays:
+            copy(array, b, 7, 0, core).wait_recv()
+
+    right, left = device(z + 1, y, x, c), device(z - 1, y, x, c)
+    u, v = device(z, uy, ux, c), device(z, vy, vx, c)
+    locals_ = [pltpu.make_async_copy(a[0], rows(a, own), a[2]) for a in arrays]
 
     @pl.when(z < 3)
     def _():
-        send_right(own, x_ref, z)
+        send(own, 3, z, right, True)
 
     @pl.when(z > 0)
     def _():
-        send_left(own, x_ref, z)
-
-    send_u(own, x_ref, z)
-    send_v(own, x_ref, z)
-    send_core(own, x_ref, z)
+        send(own, 4, z, left, True)
+
+    send(own, 5, z, u, True)
+    send(own, 6, z, v, True)
+    send(own, 7, z, core, True)
+    for local in locals_:
+        local.start()
+
+    def near(step):
+        def from_low(low):
+            return jnp.where((low == 1) & (step < 2), 1 - step, step)
+
+        return jnp.where(z < 2, from_low(z), 3 - from_low(3 - z))
 
     def got_line(at):
         b = block(at, y, x, c)
@@ -359,96 +375,91 @@
 
         @pl.when((at < z) & (z < 3))
         def _():
-            send_right(b, rows(b), at)
+            send(b, 3, at, right)
 
         @pl.when((at > z) & (z > 0))
         def _():
-            send_left(b, rows(b), at)
-
-        send_u(b, rows(b), at)
-        send_v(b, rows(b), at)
-        send_core(b, rows(b), at)
+            send(b, 4, at, left)
+
+        send(b, 5, at, u)
+        send(b, 6, at, v)
+        send(b, 7, at, core)
 
     def got_u(at):
         b = block(at, uy, ux, c)
         arrived(b)
-        send_v(b, rows(b), 4 + at)
-        send_core(b, rows(b), 4 + at)
+        send(b, 6, 4 + at, v)
+        send(b, 7, 4 + at, core)
 
     def got_v(at):
         b = block(at, vy, vx, c)
         arrived(b)
-        send_core(b, rows(b), 8 + at)
+        send(b, 7, 8 + at, core)
 
     def got_uv(at):
         b = block(at, 1 - y, 1 - x, c)
         arrived(b)
-        send_core(b, rows(b), 12 + at)
-
-    def around(step, distance):
+        send(b, 7, 12 + at, core)
+
+    def meanwhile(step):
+        if ahead is not None:
+            ahead(step)
+
+    def around(event, distance):
         for side in (-1, 1) if distance else (0,):
             at = z + side * distance
-            pl.when((at >= 0) & (at < 4))(functools.partial(step, at))
-
-    for distance in range(4):
-        if distance:
-            around(got_line, distance)
-        around(got_u, distance)
-    for distance in range(4):
-        around(got_v, distance)
-        around(got_uv, distance)
+            pl.when((at >= 0) & (at < 4))(functools.partial(event, at))
+
+    for distance in range(1, 4):
+        around(got_line, distance)
+        meanwhile(2 * distance - 2)
+        around(got_u, distance - 1)
+        meanwhile(2 * distance - 1)
+    around(got_u, 3)
+    meanwhile(6)
+    for local in locals_:
+        local.wait()
+
+    @pl.loop(0, 4)
+    def _(step):
+        at = near(step)
+        got_v(at)
+        meanwhile(7 + 3 * step)
+        got_uv(at)
+        meanwhile(8 + 3 * step)
+
+        @pl.loop(0, 4)
+        def _(i):
+            arrived(at * 8 + i * 2 + 1 - c)
+
+        meanwhile(9 + 3 * step)
+
+        if work is not None:
+            work(at)
+
+    def sent(kind, i):
+        for array in arrays:
+            copy(array, own, kind, i, core).wait_send()
 
     @pl.loop(0, 16)
     def _(i):
-        arrived((i // 2) * 4 + (i % 2) * 2 + 1 - c)
-
-    local.wait()
-
-    def sent(sem):
-        copy(own, x_ref, sem, device(z, y, x, 1 - c)).wait_send()
-
-    @pl.loop(0, 16)
-    def _(i):
-        sent(core_sem.at[i])
+        sent(7, i)
 
     @pl.loop(0, 8)
     def _(i):
-        sent(v_sem.at[i])
+        sent(6, i)
 
     @pl.loop(0, 4)
     def _(i):
-        sent(u_sem.at[i])
+        sent(5, i)
 
         @pl.when((i <= z) & (z < 3))
         def _():
-            sent(right_sem.at[i])
+            sent(3, i)
 
         @pl.when((i >= z) & (z > 0))
         def _():
-            sent(left_sem.at[i])
-
-
-def gather_kernel(*refs):
-    greet_grid()
-    n = len(GATHER_SEMS)
-    arrays = len(refs) // (n + 2)
-    for a in range(arrays):
-        gather_steps(refs[a], refs[arrays + a], *refs[2 * arrays + a * n : 2 * arrays + (a + 1) * n])
-
-
-def gather32(arrays, spare, cid):
-    return pl.pallas_call(
-        gather_kernel,
-        out_shape=[
-            jax.ShapeDtypeStruct((32 * a.shape[0] + e, a.shape[1]), a.dtype)
-            for a, e in zip(arrays, spare)
-        ],
-        in_specs=[ANY] * len(arrays),
-        out_specs=[ANY] * len(arrays),
-        scratch_shapes=GATHER_SEMS * len(arrays),
-        compiler_params=pltpu.CompilerParams(collective_id=cid, has_side_effects=True),
-        name="gather32",
-    )(*arrays)
+            sent(4, i)
 
 
 def table_kernel(x_ref, o_ref, send_sem, recv_sem):
@@ -531,9 +542,18 @@
 
 def pack_kernel(
     p_ref,
-    o_ref,
+    w_ref,
+    wt_ref,
+    bias_ref,
+    bias_t_ref,
+    gain_ref,
+    shift_ref,
+    own,
+    act_ref,
+    kv_ref,
+    qkvt_ref,
+    x_all,
     acc,
-    own,
     y_out,
     y_in,
     r_out,
@@ -549,10 +569,29 @@
     *gather_sems,
 ):
     z, y, x, c = coords()
+    size = own.shape[0]
+    local = kv_ref.shape[1] // 2
     greet_grid()
 
     def piece(zp, yp):
         return p_ref[zp * 2 + yp].astype(jnp.float32)
+
+    def project(at):
+        @pl.loop(0, 8)
+        def _(i):
+            r = pl.ds(pl.multiple_of(at * 8 * size + i * size, size), size)
+            _, _, pre = layer_norm(x_all[r, :].astype(jnp.float32), gain_ref[...], shift_ref[...])
+            act_ref[r, :] = pre.astype(jnp.bfloat16)
+
+        @pl.loop(0, 2)
+        def _(i):
+            r = pl.ds(pl.multiple_of(at * 8 * size + i * 4 * size, 4 * size), 4 * size)
+            act = act_ref[r, :]
+            kv_ref[r, :] = (dot_nn(act, w_ref[:, local:]) + bias_ref[:, local:]).astype(jnp.bfloat16)
+            for j in range(3):
+                cols = slice(j * local, (j + 1) * local)
+                out = (dot_nt(wt_ref[cols, :], act) + bias_t_ref[cols, :]).astype(jnp.bfloat16)
+                qkvt_ref[cols, r] = out * jnp.bfloat16(HD**-0.5) if j == 0 else out
 
     def y_copy(i):
         return pltpu.make_async_remote_copy(
@@ -674,22 +713,29 @@
             def _(i=zp * 2 + yp):
                 l_copy(i).wait_send()
 
-    gather_steps(own, o_ref, *gather_sems)
-
-
-def pack_gather(parts, cid):
+    gather_steps([own], [x_all], gather_sems, project)
+
+
+def pack_gather(parts, joined, bias, gain, shift, cid):
     _, size, width = parts.shape
     bf16 = jnp.bfloat16
+    rows = 32 * size
+    total = joined.shape[1]
     slots = pltpu.VMEM((8, size, width), bf16)
     quarter = pltpu.VMEM((4, size, width), bf16)
     return pl.pallas_call(
         pack_kernel,
-        out_shape=jax.ShapeDtypeStruct((32 * size, width), bf16),
-        in_specs=[VMEM],
-        out_specs=ANY,
+        out_shape=(
+            jax.ShapeDtypeStruct((size, width), bf16),
+            jax.ShapeDtypeStruct((rows, width), bf16),
+            jax.ShapeDtypeStruct((rows, total // 3 * 2), bf16),
+            jax.ShapeDtypeStruct((total, rows), bf16),
+        ),
+        in_specs=[VMEM] * 7,
+        out_specs=[VMEM] * 4,
         scratch_shapes=[
+            pltpu.VMEM((rows, width), bf16),
             pltpu.VMEM((size, width), jnp.float32),
-            pltpu.VMEM((size, width), bf16),
             quarter,
             quarter,
             slots,
@@ -705,17 +751,37 @@
         ]
         + GATHER_SEMS,
         compiler_params=pltpu.CompilerParams(
-            collective_id=cid, has_side_effects=True, vmem_limit_bytes=40 << 20
+            collective_id=cid, has_side_effects=True, vmem_limit_bytes=58 << 20
         ),
+        cost_estimate=cost(90),
         name="pack_gather",
-    )(parts)
-
-
-def share_kernel(p_ref, o_ref, landed, send_sem, recv_sem):
+    )(parts, joined, joined.T, bias[None], bias[:, None], gain[None], shift[None])
+
+
+def greet_all():
+    z, y, x, c = coords()
+    barrier = pltpu.get_barrier_semaphore()
+
+    def signal(peer):
+        pl.semaphore_signal(barrier, inc=1, device_id=peer, device_id_type=MESH)
+
+    @pl.when(z > 0)
+    def _():
+        signal(device(z - 1, y, x, c))
+
+    @pl.when(z < 3)
+    def _():
+        signal(device(z + 1, y, x, c))
+
+    signal(device(z, 1 - y, x, c))
+    for peer in (device(z, y, 1 - x, c), device(z, y, x, 1 - c), device(z, y, 1 - x, 1 - c)):
+        signal(peer)
+    pl.semaphore_wait(barrier, 4 + jnp.minimum(z, 1) + jnp.minimum(3 - z, 1))
+
+
+def share_start(p_ref, landed, send_sem, recv_sem):
     dp = lax.axis_index("dp")
     t = lax.axis_index("tensor")
-    peers = [lax.rem(t + s, 4) for s in (2, 3, 1)]
-    greet([(dp, peer) for peer in peers])
     copies = [
         pltpu.make_async_remote_copy(
             src_ref=p_ref.at[peer],
@@ -725,33 +791,254 @@
             device_id=(dp, peer),
             device_id_type=MESH,
         )
-        for s, peer in enumerate(peers)
+        for s, peer in enumerate([lax.rem(t + s, 4) for s in (2, 3, 1)])
     ]
     for copy in copies:
         copy.start()
-    total = p_ref[t].astype(jnp.float32)
+    return copies
+
+
+def share_sum(p_ref, landed, copies):
+    total = p_ref[lax.axis_index("tensor")].astype(jnp.float32)
     for s, copy in enumerate(copies):
         copy.wait_recv()
         total += landed[s].astype(jnp.float32)
-    o_ref[...] = total
     for copy in copies:
         copy.wait_send()
-
-
-def share4(parts, cid):
-    rows, width = parts.shape
-    size = rows // 4
+    return total
+
+
+def share_scratch(size, width):
+    return [pltpu.VMEM((3, size, width), jnp.bfloat16), DMA((3,)), DMA((3,))]
+
+
+def load_all(sources, targets, sems):
+    copies = [
+        pltpu.make_async_copy(a, b, sems.at[i]) for i, (a, b) in enumerate(zip(sources, targets))
+    ]
+    for copy in copies:
+        copy.start()
+    return copies
+
+
+def products(units):
+    total = sum(count for _, count in units)
+    each = (total + 9) // 10
+
+    def ahead(step):
+        @pl.when(step < 10)
+        def _():
+            @pl.loop(0, each)
+            def _(i):
+                job = step * each + i
+                before = 0
+                for unit, count in units:
+                    pl.when((job >= before) & (job < before + count))(
+                        functools.partial(unit, job - before)
+                    )
+                    before += count
+
+    return ahead
+
+
+def outer_unit(a, b, out, tall, wide):
+    across = b.shape[1] // wide
+
+    def unit(job):
+        n = pl.ds(pl.multiple_of(lax.rem(job, across) * wide, 128), wide)
+        if tall == a.shape[1]:
+            out[:, n] = dot_tn(a[...], b[:, n])
+        else:
+            m = pl.ds(pl.multiple_of(job // across * tall, 128), tall)
+            out[m, n] = dot_tn(a[:, m], b[:, n])
+
+    return unit, a.shape[1] // tall * across
+
+
+def first_kernel(p_ref, x_ref, bias_ref, gain_ref, shift_ref, mid_ref, o_ref, own, landed, ss, sr, *sems):
+    greet_all()
+    copies = share_start(p_ref, landed, ss, sr)
+    middle = x_ref[...].astype(jnp.float32) + share_sum(p_ref, landed, copies) + bias_ref[...]
+    mid_ref[...] = middle
+    _, _, pre = layer_norm(middle, gain_ref[...], shift_ref[...])
+    own[...] = pre.astype(jnp.bfloat16)
+    gather_steps([own], [o_ref], sems)
+
+
+def first_exchange(part, source, bias_out, gain2, shift2, cid):
+    size, width = source.shape
     return pl.pallas_call(
-        share_kernel,
-        out_shape=jax.ShapeDtypeStruct((size, width), jnp.float32),
-        in_specs=[VMEM],
-        out_specs=VMEM,
-        scratch_shapes=[pltpu.VMEM((3, size, width), parts.dtype), DMA((3,)), DMA((3,))],
+        first_kernel,
+        out_shape=(
+            jax.ShapeDtypeStruct((size, width), jnp.float32),
+            jax.ShapeDtypeStruct((32 * size, width), jnp.bfloat16),
+        ),
+        in_specs=[VMEM] * 5,
+        out_specs=[VMEM, ANY],
+        scratch_shapes=[pltpu.VMEM((size, width), jnp.bfloat16)]
+        + share_scratch(size, width)
+        + GATHER_SEMS,
         compiler_params=pltpu.CompilerParams(
             collective_id=cid, has_side_effects=True, vmem_limit_bytes=24 << 20
         ),
-        name="share4",
-    )(parts.reshape(4, size, width))
+        cost_estimate=cost(60),
+        name="first_exchange",
+    )(part.reshape(4, size, width), source, bias_out[None], gain2[None], shift2[None])
+
+
+def second_kernel(
+    p_ref, b_ref, mid_ref, up_ref, gain_ref, bias_ref, wout_ref, act_ref, hid_ref, dpre_ref, upall_ref,
+    dmid_ref, mixed_ref, vec_ref, o_ref, gup_ref, gdown_ref, dctx_ref, gbias_ref,
+    own, landed, ss, sr, landed2, ss2, sr2, some, act, hid, dpre, upall, load_sem, *sems,
+):
+    loads = load_all((act_ref, dpre_ref, hid_ref, upall_ref), (act, dpre, hid, upall), load_sem)
+    greet_all()
+    copies = share_start(p_ref, landed, ss, sr)
+    branch_copies = share_start(b_ref, landed2, ss2, sr2)
+    grad = share_sum(p_ref, landed, copies)
+    middle = mid_ref[...]
+    normed, rstd, _ = layer_norm(middle, 1.0, 0.0)
+    d_middle = up_ref[...].astype(jnp.float32) + layer_norm_back(grad, normed, rstd, gain_ref[...])
+    own[...] = d_middle.astype(jnp.bfloat16)
+    dmid_ref[...] = d_middle
+    vec_ref[...] = jnp.concatenate(
+        [
+            jnp.sum(grad * normed, 0, keepdims=True),
+            jnp.sum(grad, 0, keepdims=True),
+            jnp.zeros((6, grad.shape[1]), jnp.float32),
+        ],
+        0,
+    )
+    work = products([outer_unit(act, dpre, gup_ref, 256, 1280), outer_unit(hid, upall, gdown_ref, 256, 1280)])
+
+    def ahead(step):
+        @pl.when(step == 0)
+        def _():
+            branch = share_sum(b_ref, landed2, branch_copies)
+            mixed_ref[...] = (mid_ref[...] + branch + bias_ref[...]).astype(jnp.bfloat16)
+            for load in loads:
+                load.wait()
+
+        work(step)
+
+    size = own.shape[0]
+    gbias_ref[...] = jnp.zeros_like(gbias_ref)
+
+    def context_grad(at):
+        @pl.loop(0, 2)
+        def _(i):
+            r = pl.ds(pl.multiple_of(at * 8 * size + i * 4 * size, 4 * size), 4 * size)
+            pltpu.sync_copy(o_ref.at[r], some)
+            dctx_ref[:, r] = dot_nt(wout_ref[...], some[...]).astype(jnp.bfloat16)
+            gbias_ref[0:1, :] += jnp.sum(some[...].astype(jnp.float32), 0, keepdims=True)
+
+    gather_steps([own], [o_ref], sems, context_grad, ahead)
+
+
+def second_exchange(part, branch, middle, upstream, gain2, bias_down, w_out, act2, hidden, d_pre, up_all, cid):
+    size, width = middle.shape
+    f32, bf16 = jnp.float32, jnp.bfloat16
+    rows, inner = hidden.shape
+    return pl.pallas_call(
+        second_kernel,
+        out_shape=(
+            jax.ShapeDtypeStruct((size, width), f32),
+            jax.ShapeDtypeStruct((size, width), bf16),
+            jax.ShapeDtypeStruct((8, width), f32),
+            jax.ShapeDtypeStruct((rows, width), bf16),
+            jax.ShapeDtypeStruct((width, inner), f32),
+            jax.ShapeDtypeStruct((inner, width), f32),
+            jax.ShapeDtypeStruct((w_out.shape[0], rows), bf16),
+            jax.ShapeDtypeStruct((8, width), f32),
+        ),
+        in_specs=[VMEM] * 7 + [ANY] * 4,
+        out_specs=[VMEM, VMEM, VMEM, ANY, VMEM, VMEM, VMEM, VMEM],
+        scratch_shapes=[pltpu.VMEM((size, width), bf16)]
+        + share_scratch(size, width) * 2
+        + [pltpu.VMEM((4 * size, width), bf16)]
+        + [pltpu.VMEM((rows, n), bf16) for n in (width, inner, inner, width)]
+        + [DMA((4,))]
+        + GATHER_SEMS,
+        compiler_params=pltpu.CompilerParams(
+            collective_id=cid, has_side_effects=True, vmem_limit_bytes=60 << 20
+        ),
+        cost_estimate=cost(80),
+        name="second_exchange",
+    )(
+        part.reshape(4, size, width), branch.reshape(4, size, width), middle, upstream,
+        gain2[None], bias_down[None], w_out, act2, hidden, d_pre, up_all,
+    )
+
+
+def third_kernel(
+    p_ref, x_ref, dmid_ref, gain_ref, vec_ref, act_ref, dt_ref, ctx_ref, dmall_ref,
+    o_ref, vo_ref, gqkv_ref, gout_ref,
+    own, vec, landed, ss, sr, act, dt, ctx, dmall, load_sem, *sems,
+):
+    loads = load_all((act_ref, dt_ref, ctx_ref, dmall_ref), (act, dt, ctx, dmall), load_sem)
+    greet_all()
+    copies = share_start(p_ref, landed, ss, sr)
+    grad = share_sum(p_ref, landed, copies)
+    normed, rstd, _ = layer_norm(x_ref[...].astype(jnp.float32), 1.0, 0.0)
+    own[...] = (dmid_ref[...] + layer_norm_back(grad, normed, rstd, gain_ref[...])).astype(jnp.bfloat16)
+    vec[...] = jnp.concatenate(
+        [
+            vec_ref[0:2, :],
+            jnp.sum(grad * normed, 0, keepdims=True),
+            jnp.sum(grad, 0, keepdims=True),
+            jnp.zeros((4, grad.shape[1]), jnp.float32),
+        ],
+        0,
+    )
+    part = dt.shape[0] // 3
+
+    def project(job):
+        m = pl.ds(pl.multiple_of(job // 3 * 256, 256), 256)
+        k = lax.rem(job, 3)
+        gqkv_ref[k, m, :] = dot_nn(dt[pl.ds(pl.multiple_of(k * part, 64), part), :], act[:, m]).T
+
+    work = products([(project, act.shape[1] // 256 * 3), outer_unit(ctx, dmall, gout_ref, part, 640)])
+
+    def ahead(step):
+        @pl.when(step == 0)
+        def _():
+            for load in loads:
+                load.wait()
+
+        work(step)
+
+    gather_steps([own, vec], [o_ref, vo_ref], sems, ahead=ahead)
+
+
+def third_exchange(part, source, d_middle, gain1, vec, act1, d_qkv, context, d_middle_all, cid):
+    size, width = d_middle.shape
+    f32, bf16 = jnp.float32, jnp.bfloat16
+    rows = act1.shape[0]
+    total = d_qkv.shape[0]
+    return pl.pallas_call(
+        third_kernel,
+        out_shape=(
+            jax.ShapeDtypeStruct((rows, width), bf16),
+            jax.ShapeDtypeStruct((256, width), f32),
+            jax.ShapeDtypeStruct((3, width, total // 3), f32),
+            jax.ShapeDtypeStruct((total // 3, width), f32),
+        ),
+        in_specs=[VMEM] * 5 + [ANY] * 4,
+        out_specs=[ANY, ANY, VMEM, VMEM],
+        scratch_shapes=[pltpu.VMEM((size, width), bf16), pltpu.VMEM((8, width), f32)]
+        + share_scratch(size, width)
+        + [pltpu.VMEM(a.shape, bf16) for a in (act1, d_qkv, context, d_middle_all)]
+        + [DMA((4,))]
+        + GATHER_SEMS * 2,
+        compiler_params=pltpu.CompilerParams(
+            collective_id=cid, has_side_effects=True, vmem_limit_bytes=60 << 20
+        ),
+        cost_estimate=cost(60),
+        name="third_exchange",
+    )(
+        part.reshape(4, size, width), source, d_middle, gain1[None], vec,
+        act1, d_qkv, context, d_middle_all,
+    )
 
 
 def dot_nt(a, b):
@@ -762,26 +1049,47 @@
     return lax.dot_general(a, b, (((1,), (0,)), ((), ())), preferred_element_type=jnp.float32)
 
 
-def attend_kernel(heads, klo, khi, qkv_ref, vt_ref, seg_ref, ctx_ref, lse_ref, m_s, l_s, acc_s):
-    i = pl.program_id(0)
-    q0 = pl.multiple_of(i * BQ, BQ)
+def dot_tn(a, b):
+    return lax.dot_general(a, b, (((0,), (0,)), ((), ())), preferred_element_type=jnp.float32)
+
+
+def spans(offset_ref, length_ref, first, count):
+    row = lax.broadcasted_iota(jnp.int32, (1, count), 1) + first
+    start = jnp.zeros((1, count), jnp.int32)
+    end = jnp.zeros((1, count), jnp.int32)
+    low, high = 1 << 20, 0
+    for i in range(offset_ref.shape[0]):
+        a = offset_ref[i]
+        b = a + length_ref[i]
+        inside = (row >= a) & (row < b)
+        start = jnp.where(inside, a, start)
+        end = jnp.where(inside, b, end)
+        used = (a < first + count) & (b > first) & (b > a)
+        low = jnp.where(used, jnp.minimum(low, a // BK), low)
+        high = jnp.where(used, jnp.maximum(high, (b + BK - 1) // BK), high)
+    return start, end, low, high
+
+
+def attend_kernel(heads, offset_ref, length_ref, qkvt_ref, kv_ref, ctx_ref, lse_ref, m_s, l_s, acc_s):
+    rows = ctx_ref.shape[0]
     local = heads * HD
     span = range(heads)
-    start = seg_ref[0:1, pl.ds(q0, BQ)]
-    end = seg_ref[1:2, pl.ds(q0, BQ)]
+    first = lax.axis_index("dp") * rows
+    mine = pl.ds(pl.multiple_of(first, 128), rows)
+    start, end, low, high = spans(offset_ref, length_ref, first, rows)
     m_s[...] = jnp.full_like(m_s, NEG)
     l_s[...] = jnp.zeros_like(l_s)
     acc_s[...] = jnp.zeros_like(acc_s)
-    q = [qkv_ref[pl.ds(q0, BQ), h * HD : (h + 1) * HD] for h in span]
+    q = [qkvt_ref[h * HD : (h + 1) * HD, mine] for h in span]
 
     def body(kb, carry):
         k0 = pl.multiple_of(kb * BK, BK)
-        key = lax.broadcasted_iota(jnp.int32, (BK, BQ), 0) + k0
+        key = lax.broadcasted_iota(jnp.int32, (BK, rows), 0) + k0
         mask = (key >= start) & (key < end)
         s = [
             jnp.where(
                 mask,
-                dot_nt(qkv_ref[pl.ds(k0, BK), local + h * HD : local + (h + 1) * HD], q[h]),
+                dot_nn(kv_ref[pl.ds(k0, BK), h * HD : (h + 1) * HD], q[h]),
                 NEG,
             )
             for h in span
@@ -797,146 +1105,171 @@
             p.append(e.astype(jnp.bfloat16))
             a.append(scale)
         for h in span:
-            vt = vt_ref[h * HD : (h + 1) * HD, pl.ds(k0, BK)]
+            vt = qkvt_ref[2 * local + h * HD : 2 * local + (h + 1) * HD, pl.ds(k0, BK)]
             acc_s[h] = a[h] * acc_s[h] + dot_nn(vt, p[h])
         return carry
 
-    lax.fori_loop(klo[i], khi[i], body, 0)
+    lax.fori_loop(low, high, body, 0)
+    parts = [[], [], []]
     for h in span:
         total = l_s[h]
         total = jnp.where(total == 0.0, 1.0, total)
-        lse_ref[h : h + 1, :] = m_s[h] + jnp.log(total)
+        rest = m_s[h] + jnp.log(total)
+        for part in parts:
+            part.append(rest.astype(jnp.bfloat16).astype(jnp.float32))
+            rest = rest - part[-1]
         out = acc_s[h] * (1.0 / total)
         ctx_ref[:, h * HD : (h + 1) * HD] = out.T.astype(jnp.bfloat16)
+    blank = [jnp.zeros((128 - 3 * heads, rows), jnp.float32)]
+    lse_ref[...] = jnp.concatenate(parts[0] + parts[1] + parts[2] + blank, 0).T.astype(jnp.bfloat16)
 
 
 def whole(a):
     return pl.BlockSpec(a.shape, lambda i, *_: (0,) * len(a.shape), pipeline_mode=pl.Buffered(1))
 
 
-def attend(qkv, vt, seg, klo, khi, heads):
-    rows = qkv.shape[0]
+def attend(qkvt, kv, offsets, lengths, heads):
+    rows = kv.shape[0] // 8
     local = heads * HD
-    row = pltpu.VMEM((heads, 1, BQ), jnp.float32)
+    row = pltpu.VMEM((heads, 1, rows), jnp.float32)
     return pl.pallas_call(
         functools.partial(attend_kernel, heads),
         out_shape=(
             jax.ShapeDtypeStruct((rows, local), jnp.bfloat16),
-            jax.ShapeDtypeStruct((8, rows), jnp.float32),
+            jax.ShapeDtypeStruct((rows, 128), jnp.bfloat16),
         ),
-        grid_spec=pltpu.PrefetchScalarGridSpec(
-            num_scalar_prefetch=2,
-            grid=(rows // BQ,),
-            in_specs=[whole(qkv), whole(vt), whole(seg)],
-            out_specs=[
-                pl.BlockSpec((BQ, local), lambda i, *_: (i, 0)),
-                pl.BlockSpec((8, BQ), lambda i, *_: (0, i)),
-            ],
-            scratch_shapes=[row, row, pltpu.VMEM((heads, HD, BQ), jnp.float32)],
-        ),
+        in_specs=[SMEM, SMEM] + [VMEM] * 2,
+        out_specs=[VMEM, VMEM],
+        scratch_shapes=[row, row, pltpu.VMEM((heads, HD, rows), jnp.float32)],
         compiler_params=pltpu.CompilerParams(vmem_limit_bytes=40 << 20),
+        cost_estimate=cost(10),
         name="attend",
-    )(klo, khi, qkv, vt, seg)
+    )(offsets, lengths, qkvt, kv)
 
 
 def attend_back_kernel(
-    heads, klo, khi, qkv_ref, kt_ref, do_ref, ctx_ref, lse_ref, seg_ref, d_ref, dbq_ref, dbv_ref, dk_s, dv_s, dq_s
+    heads, offset_ref, length_ref, kv_ref, qkt_ref, dot_ref, ctxt_ref, lse_ref, d_ref, dk_s, dv_s, dq_s
 ):
     i = pl.program_id(0)
-    n = pl.num_programs(0)
-    q0 = pl.multiple_of(i * BQ, BQ)
     local = heads * HD
     span = range(heads)
+    sl = [slice(h * HD, (h + 1) * HD) for h in span]
+    at_q = pl.ds(pl.multiple_of(i * BQ, BQ), BQ)
 
     @pl.when(i == 0)
     def _():
         dk_s[...] = jnp.zeros_like(dk_s)
         dv_s[...] = jnp.zeros_like(dv_s)
-        dbq_ref[...] = jnp.zeros_like(dbq_ref)
-        dbv_ref[...] = jnp.zeros_like(dbv_ref)
-
-    start = seg_ref[0:1, pl.ds(q0, BQ)]
-    end = seg_ref[1:2, pl.ds(q0, BQ)]
+
+    start, end, low, high = spans(offset_ref, length_ref, i * BQ, BQ)
     dq_s[...] = jnp.zeros_like(dq_s)
     delta = []
     for h in span:
-        sl = slice(h * HD, (h + 1) * HD)
-        both = do_ref[pl.ds(q0, BQ), sl].astype(jnp.float32) * ctx_ref[pl.ds(q0, BQ), sl].astype(jnp.float32)
-        delta.append(jnp.sum(both.T, 0, keepdims=True))
+        both = dot_ref[sl[h], at_q].astype(jnp.float32) * ctxt_ref[sl[h], at_q].astype(jnp.float32)
+        delta.append(jnp.sum(both, 0, keepdims=True))
 
     def body(kb, carry):
-        k0 = pl.multiple_of(kb * BK, BK)
-        key = lax.broadcasted_iota(jnp.int32, (BK, BQ), 0) + k0
+        at_k = pl.ds(pl.multiple_of(kb * BK, BK), BK)
+        key = lax.broadcasted_iota(jnp.int32, (BK, BQ), 0) + kb * BK
         mask = (key >= start) & (key < end)
-        q = [qkv_ref[pl.ds(q0, BQ), h * HD : (h + 1) * HD] for h in span]
-        do = [do_ref[pl.ds(q0, BQ), h * HD : (h + 1) * HD] for h in span]
-        s = [
-            dot_nt(qkv_ref[pl.ds(k0, BK), local + h * HD : local + (h + 1) * HD], q[h])
-            for h in span
-        ]
-        dp = [
-            dot_nt(qkv_ref[pl.ds(k0, BK), 2 * local + h * HD : 2 * local + (h + 1) * HD], do[h])
-            for h in span
-        ]
-        p = [
-            jnp.exp(jnp.where(mask, s[h], NEG) - lse_ref[h : h + 1, pl.ds(q0, BQ)]) for h in span
-        ]
-        ds = [(p[h] * (dp[h] - delta[h])).astype(jnp.bfloat16) for h in span]
-        pb = [p[h].astype(jnp.bfloat16) for h in span]
+
+        def products(h):
+            s = dot_nn(kv_ref[at_k, sl[h]], qkt_ref[sl[h], at_q])
+            dp = dot_nn(kv_ref[at_k, local + h * HD : local + (h + 1) * HD], dot_ref[sl[h], at_q])
+            return s, dp
+
+        def scores(h, s, dp):
+            p = jnp.exp(jnp.where(mask, s, NEG) - lse_ref[h : h + 1, at_q])
+            ds = (p * (dp - delta[h])).astype(jnp.bfloat16)
+            return p.astype(jnp.bfloat16), ds
+
+        def gradients(h, p, ds):
+            dv_s[h, :, at_k] += dot_nt(dot_ref[sl[h], at_q], p)
+            dk_s[h, :, at_k] += dot_nt(qkt_ref[sl[h], at_q], ds)
+            dq_s[h] += dot_nn(qkt_ref[local + h * HD : local + (h + 1) * HD, at_k], ds)
+
+        now = products(0)
+        held = None
         for h in span:
-            dv_s[h, pl.ds(k0, BK), :] += dot_nn(pb[h], do[h])
-        for h in span:
-            dk_s[h, pl.ds(k0, BK), :] += dot_nn(ds[h], q[h])
-        for h in span:
-            dq_s[h] += dot_nn(kt_ref[h * HD : (h + 1) * HD, pl.ds(k0, BK)], ds[h])
+            later = products(h + 1) if h + 1 < heads else None
+            done = scores(h, *now)
+            if held is not None:
+                gradients(h - 1, *held)
+            held, now = done, later
+        gradients(heads - 1, *held)
         return carry
 
-    lax.fori_loop(klo[i], khi[i], body, 0)
+    lax.fori_loop(low, high, body, 0)
     for h in span:
-        dq = dq_s[h].T * 0.125
-        d_ref[pl.ds(q0, BQ), h * HD : (h + 1) * HD] = dq.astype(jnp.bfloat16)
-        dbq_ref[h : h + 1, :] += jnp.sum(dq, 0, keepdims=True)
-
-    @pl.when(i == n - 1)
+        d_ref[sl[h], at_q] = (dq_s[h] * HD**-0.5).astype(jnp.bfloat16)
+
+    @pl.when(i == pl.num_programs(0) - 1)
     def _():
         for h in span:
-
-            def finish(j, carry):
-                r = pl.ds(pl.multiple_of(j * BK, BK), BK)
-                dk = dk_s[h, r, :]
-                dv = dv_s[h, r, :]
-                d_ref[r, local + h * HD : local + (h + 1) * HD] = dk.astype(jnp.bfloat16)
-                d_ref[r, 2 * local + h * HD : 2 * local + (h + 1) * HD] = dv.astype(jnp.bfloat16)
-                return carry + jnp.sum(dv, 0, keepdims=True)
-
-            dbv_ref[h : h + 1, :] = lax.fori_loop(0, n, finish, jnp.zeros((1, HD), jnp.float32))
-
-
-def attend_back(qkv, kt, do, ctx, lse, seg, klo, khi, heads):
-    rows = qkv.shape[0]
+            d_ref[local + h * HD : local + (h + 1) * HD, :] = dk_s[h].astype(jnp.bfloat16)
+            d_ref[2 * local + h * HD : 2 * local + (h + 1) * HD, :] = dv_s[h].astype(jnp.bfloat16)
+
+
+def attend_back(kv, qkt, dot, ctxt, lse, offsets, lengths, heads):
+    rows = kv.shape[0]
     local = heads * HD
-
-    def const(shape):
-        return pl.BlockSpec(shape, lambda i, *_: (0, 0), pipeline_mode=pl.Buffered(1))
-
-    tall = pltpu.VMEM((heads, rows, HD), jnp.float32)
+    tall = pltpu.VMEM((heads, HD, rows), jnp.float32)
     return pl.pallas_call(
         functools.partial(attend_back_kernel, heads),
-        out_shape=(
-            jax.ShapeDtypeStruct((rows, 3 * local), jnp.bfloat16),
-            jax.ShapeDtypeStruct((8, HD), jnp.float32),
-            jax.ShapeDtypeStruct((8, HD), jnp.float32),
-        ),
+        out_shape=jax.ShapeDtypeStruct((3 * local, rows), jnp.bfloat16),
         grid_spec=pltpu.PrefetchScalarGridSpec(
             num_scalar_prefetch=2,
             grid=(rows // BQ,),
-            in_specs=[whole(qkv), whole(kt), whole(do), whole(ctx), whole(lse), whole(seg)],
-            out_specs=[const((rows, 3 * local)), const((8, HD)), const((8, HD))],
+            in_specs=[whole(a) for a in (kv, qkt, dot, ctxt, lse)],
+            out_specs=pl.BlockSpec(
+                (3 * local, rows), lambda i, *_: (0, 0), pipeline_mode=pl.Buffered(1)
+            ),
             scratch_shapes=[tall, tall, pltpu.VMEM((heads, HD, BQ), jnp.float32)],
         ),
-        compiler_params=pltpu.CompilerParams(vmem_limit_bytes=60 << 20),
+        compiler_params=pltpu.CompilerParams(vmem_limit_bytes=48 << 20),
+        cost_estimate=cost(60),
         name="attend_back",
-    )(klo, khi, qkv, kt, do, ctx, lse, seg)
+    )(offsets, lengths, kv, qkt, dot, ctxt, lse)
+
+
+def unpack_kernel(info_ref, m_ref, d_ref, mo_ref, do_ref, m, d, sems):
+    cap = mo_ref.shape[0]
+    rows = m_ref.shape[0]
+    offset = info_ref[0]
+    length = info_ref[1]
+    first = pl.multiple_of(jnp.minimum(offset, rows - cap), 16)
+    loads = [
+        pltpu.make_async_copy(src.at[pl.ds(first, cap)], dst.at[pl.ds(0, cap)], sems.at[i])
+        for i, (src, dst) in enumerate(((m_ref, m), (d_ref, d)))
+    ]
+    for load in loads:
+        load.start()
+    for load, src, dst in zip(loads, (m, d), (mo_ref, do_ref)):
+        load.wait()
+
+        @pl.loop(0, cap // 128)
+        def _(i):
+            at = pl.multiple_of(jnp.minimum(offset - first + i * 128, cap), 16)
+            row = lax.broadcasted_iota(jnp.int32, (128, 1), 0) + i * 128
+            value = jnp.where(row < length, src[pl.ds(at, 128), :].astype(jnp.float32), 0.0)
+            dst[pl.ds(pl.multiple_of(i * 128, 128), 128), :] = value.astype(dst.dtype)
+
+
+def unpack(info, mixed, d_tokens, cap):
+    width = mixed.shape[1]
+    held = pltpu.VMEM((cap + 128, width), jnp.bfloat16)
+    return pl.pallas_call(
+        unpack_kernel,
+        out_shape=(
+            jax.ShapeDtypeStruct((cap, width), jnp.bfloat16),
+            jax.ShapeDtypeStruct((cap, width), jnp.float32),
+        ),
+        in_specs=[SMEM, ANY, ANY],
+        out_specs=[VMEM, VMEM],
+        scratch_shapes=[held, held, DMA((2,))],
+        compiler_params=pltpu.CompilerParams(vmem_limit_bytes=40 << 20),
+        name="unpack",
+    )(info, mixed, d_tokens)
 
 
 def packed_step(size, cids, offset, length, offsets, lengths, args):
@@ -951,44 +1284,30 @@
     rows = 32 * size
     mine = 4 * size
     dp = lax.axis_index("dp")
-    t = lax.axis_index("tensor")
-    pack_id, gather_id, share_id, last_id = cids
-
-    def own(value, count=mine, at=None):
-        first = dp * mine if at is None else at
-        return lax.dynamic_slice_in_dim(value, first, count, 0)
-
-    at_block = (dp * 4 + t) * size
+    pack_id, first_id, second_id, third_id = cids
+
+    def own(value):
+        return lax.dynamic_slice_in_dim(value, dp * mine, mine, 0)
+
     info = jnp.stack([offset, length])
     x_parts, up_parts = take_pieces(tokens, grad_out, info, size)
-    x_all = pack_gather(x_parts, pack_id)
-    up_all = pack_gather(up_parts, pack_id)
-
-    index = jnp.arange(rows, dtype=jnp.int32)
-    inside = (index[None, :] >= offsets[:, None]) & (index[None, :] < (offsets + lengths)[:, None])
-    start = jnp.sum(jnp.where(inside, offsets[:, None], 0), 0)
-    end = jnp.sum(jnp.where(inside, (offsets + lengths)[:, None], 0), 0)
-    seg = jnp.concatenate([start[None], end[None], jnp.zeros((6, rows), jnp.int32)], 0)
-    taken = end > 0
-    first_key = jnp.min(jnp.where(taken, start, rows).reshape(-1, BQ), 1)
-    last_key = jnp.max(end.reshape(-1, BQ), 1)
-    klo = jnp.where(last_key > 0, first_key // BK, 0)
-    khi = (last_key + BK - 1) // BK
-
-    _, _, pre1 = layer_norm(x_all.astype(f32), gain1, shift1)
-    act1 = pre1.astype(bf16)
     joined = w_qkv.reshape(width, 3 * local)
     bias = jnp.concatenate([bias_q, jnp.zeros_like(bias_q), bias_v])
-    scale = jnp.concatenate([jnp.full((local,), HD**-0.5, bf16), jnp.ones((2 * local,), bf16)])
-    qkv = (jnp.dot(act1, joined, preferred_element_type=f32) + bias).astype(bf16) * scale
-    context, lse = attend(qkv, qkv[:, 2 * local :].T, seg, klo, khi, heads)
-    part = jnp.dot(own(context), w_out, preferred_element_type=f32).astype(bf16)
-    attended = share4(part, share_id)
-    source = own(x_all, size, at_block).astype(f32)
-    middle = source + attended + bias_out
-    normed2, rstd2, pre2 = layer_norm(middle, gain2, shift2)
-    (act2,) = gather32([pre2.astype(bf16)], [cap], gather_id)
-    act2 = act2[:rows]
+    source, act1, kv, qkvt = pack_gather(x_parts, joined, bias, gain1, shift1, pack_id)
+    up_own = lax.psum_scatter(up_parts, "dp", scatter_dimension=0, tiled=True)
+    up_own, source = lax.optimization_barrier((up_own, source))
+    up_all = lax.all_gather(up_own.reshape(size, width), ("dp", "tensor"), tiled=True)
+
+    context_own, lse_own = attend(
+        qkvt, kv, offsets, lengths, heads
+    )
+    part = jnp.dot(context_own, w_out, preferred_element_type=f32).astype(bf16)
+    sent = jnp.concatenate([context_own, lse_own], 1)
+    sent = lax.all_gather(sent, "dp", tiled=True)
+    context = sent[:, :local]
+    lse = jnp.sum(sent[:, local : local + 3 * heads].astype(f32).reshape(rows, 3, heads), 1).T
+    lse = jnp.concatenate([lse, jnp.zeros((8 - heads, rows), f32)], 0)
+    middle, act2 = first_exchange(part, source, bias_out, gain2, shift2, first_id)
 
     pre = jnp.dot(act2, w_up, preferred_element_type=f32) + bias_up
     hidden_f, slope = gelu_pair(pre)
@@ -996,63 +1315,44 @@
     d_pre = contract_last(up_all, w_down) * slope
     g_up_bias = jnp.sum(d_pre, 0)
     d_pre_b = d_pre.astype(bf16)
-    d_act2 = share4(contract_last(own(d_pre_b), w_up).astype(bf16), share_id)
-    upstream = own(up_all, size, at_block).astype(f32)
-    d_middle = upstream + layer_norm_back(d_act2, normed2, rstd2, gain2)
-    (d_middle_b,) = gather32([d_middle.astype(bf16)], [cap], gather_id)
-    d_middle_b = d_middle_b[:rows]
-    g_down = contract_first(hidden, up_all)
-    g_up = contract_first(act2, d_pre_b)
+    d_part = contract_last(own(d_pre_b), w_up).astype(bf16)
+    branch = jnp.dot(own(hidden), w_down, preferred_element_type=f32).astype(bf16)
+    d_middle, mixed, vec, d_middle_b, g_up, g_down, d_context, g_out_bias = second_exchange(
+        d_part, branch, middle, up_own.reshape(size, width), gain2, bias_down,
+        w_out, act2, hidden, d_pre_b, up_all, second_id,
+    )
     g_down_bias = jnp.sum(up_all.astype(f32), 0)
-    branch = share4(
-        jnp.dot(own(hidden), w_down, preferred_element_type=f32).astype(bf16), share_id
-    )
-    (mixed_all,) = gather32([(middle + branch + bias_down).astype(bf16)], [cap], gather_id)
-
-    g_out_bias = jnp.sum(d_middle_b.astype(f32), 0)
-    g_out = contract_first(context, d_middle_b)
-    d_context = contract_last(d_middle_b, w_out).astype(bf16)
-    d_qkv, dbq, dbv = attend_back(
-        qkv, qkv[:, local : 2 * local].T, d_context, context, lse, seg, klo, khi, heads
-    )
-    g_bias_q = dbq[:heads].reshape(local)
-    g_bias_v = dbv[:heads].reshape(local)
-    g_qkv = contract_first(act1, d_qkv).reshape(width, 3, local)
-    d_act1 = share4(contract_last(own(d_qkv), joined).astype(bf16), share_id)
-    normed1, rstd1, _ = layer_norm(source, gain1, shift1)
-    d_tokens = d_middle + layer_norm_back(d_act1, normed1, rstd1, gain1)
-    vectors = jnp.stack(
-        [
-            jnp.sum(d_act1 * normed1, 0),
-            jnp.sum(d_act1, 0),
-            jnp.sum(d_act2 * normed2, 0),
-            jnp.sum(d_act2, 0),
-        ]
-        + [jnp.zeros((width,), f32)] * 4
-    )
-    d_tokens_all, vectors_all = gather32([d_tokens.astype(bf16), vectors], [cap, 0], last_id)
+    mixed_all = lax.all_gather(mixed, ("dp", "tensor"), tiled=True)
+    d_qkv = attend_back(
+        kv, qkvt, d_context, context.T, lse, offsets, lengths, heads
+    )
+    g_bias_q = jnp.sum(d_qkv[:local].astype(f32), 1)
+    g_bias_v = jnp.sum(d_qkv[2 * local :].astype(f32), 1)
+    d_own = lax.dynamic_slice_in_dim(d_qkv, dp * mine, mine, 1)
+    d_act1 = jnp.einsum("kr,dk->rd", d_own, joined, preferred_element_type=f32).astype(bf16)
+    d_tokens_all, vectors_all, g_qkv, g_out = third_exchange(
+        d_act1, source, d_middle, gain1, vec, act1, d_qkv, context, d_middle_b, third_id
+    )
+    g_qkv = g_qkv.transpose(1, 0, 2)
     sums = jnp.sum(vectors_all.reshape(32, 8, width), 0)
-    valid = (jnp.arange(cap, dtype=jnp.int32) < length)[:, None]
-
-    def slot(value):
-        return jnp.where(valid, own(value, cap, offset), jnp.zeros((), value.dtype))
+    mixed, d_tokens = unpack(info, mixed_all, d_tokens_all, cap)
 
     return (
-        slot(mixed_all),
-        slot(d_tokens_all).astype(f32),
+        mixed,
+        d_tokens,
         g_qkv,
         g_bias_q,
         g_bias_v,
         g_out,
-        g_out_bias,
+        g_out_bias[0],
         g_up,
         g_up_bias,
         g_down,
         g_down_bias,
+        sums[2],
+        sums[3],
         sums[0],
         sums[1],
-        sums[2],
-        sums[3],
     )
 
 
@@ -1067,7 +1367,11 @@
     table = gather_table(slot_clip[0], 0)
     match = table[:, None] == jnp.arange(clips, dtype=jnp.int32)[None, :]
     lengths = jnp.sum(jnp.where(match, clip_len[None, :], 0), 1)
-    offsets = jnp.cumsum(padded(lengths)) - padded(lengths)
+    slots = jnp.arange(8, dtype=jnp.int32)
+    ahead = (lengths[None, :] > lengths[:, None]) | (
+        (lengths[None, :] == lengths[:, None]) & (slots[None, :] < slots[:, None])
+    )
+    offsets = jnp.sum(jnp.where(ahead, padded(lengths)[None, :], 0), 1)
     dp = lax.axis_index("dp")
     length = lengths[dp]
     offset = offsets[dp]

time: 778 us -> 586 us (0.75)
  Pallas kernels: 563 us -> 444 us
  matrix products: 120 us -> 43.2 us
  local copies, waits for them, and re-layouts: 28.3 us -> 56 us
  other arithmetic: 31.4 us -> 14.4 us
    pallas_call x11 -> x6, Pallas kernels: 493 us -> 422 us  [the longest x1 129 us: pack_gather(): pl.pallas_call(pack_kernel, out_shape=(jax.ShapeDtypeStruct((size, width)...]
    dot_general x6 -> x2, matrix products: 66.9 us -> 3.98 us  [the longest x1 3.31 us: packed_step(): jnp.einsum('kr,dk->rd', d_own, joined, preferred_element_type=f32)]
    pallas_call x1, Pallas kernels: 55.9 us -> 7.01 us  [attend(): pl.pallas_call(functools.partial(attend_kernel, heads), out_shape=(jax.Sh...]
    cond x68 -> x69, local copies, waits for them, and re-layouts: 6.44 us -> 23.2 us
    unnamed x0 -> x11, local copies, waits for them, and re-layouts: none -> 14.7 us
    convert_element_type x4 -> x0, other arithmetic: 12.3 us -> none  [the longest x1 8.41 us: packed_step(): slot(d_tokens_all).astype(f32)]
    dot_general x4 -> x2, matrix products: 33.4 us -> 22.7 us  [contract_last(): lax.dot_general(left, right, (((1,), (1,)), ((), ())), preferred_element_...]
    reduce_sum x9 -> x3, other arithmetic: 12.6 us -> 3.52 us  [the longest x1 3.31 us: packed_step(): g_bias_v = jnp.sum(d_qkv[2 * local:].astype(f32), 1)]
  transfers between devices with their start and end apart: 0 -> 4, of which waited for: 0 -> 0; matrix products, arithmetic and copies ran while one was open for 0% -> 13% of each run, Pallas kernels for 0% -> 73%
where the time goes in v2:
time: 586 us; the launch traced here: 583 us
  Pallas kernels  444 us (76%)
  local copies, waits for them, and re-layouts  56 us (10%)
  matrix products  43.2 us (7%)
  between operations  15.6 us (3%)
  other arithmetic  14.4 us (2%)
  loops' own time  8.74 us (1%)
    pallas_call x1, Pallas kernels, pack_gather(): pl.pallas_call(pack_kernel, out_shape=(jax.ShapeDtypeStruct((size, width)...  129 us
    pallas_call x1, Pallas kernels, second_exchange(): pl.pallas_call(second_kernel, out_shape=(jax.ShapeDtypeStruct((size, widt...  88.5 us
    pallas_call x1, Pallas kernels, first_exchange(): pl.pallas_call(first_kernel, out_shape=(jax.ShapeDtypeStruct((size, width...  75.3 us
    pallas_call x1, Pallas kernels, third_exchange(): pl.pallas_call(third_kernel, out_shape=(jax.ShapeDtypeStruct((rows, width...  65.1 us
    pallas_call x1, Pallas kernels, attend_back(): pl.pallas_call(functools.partial(attend_back_kernel, heads), out_shape=ja...  60.5 us
    cond x69, local copies, waits for them, and re-layouts  23.2 us
    dot_general x2, matrix products, contract_last(): lax.dot_general(left, right, (((1,), (1,)), ((), ())), preferred_element_...  22.7 us
    unnamed x11, local copies, waits for them, and re-layouts  14.7 us
  transfers between devices with their start and end apart: 4, of which 0 were waited for; matrix products, arithmetic and copies ran while one was open for 13% of the time, Pallas kernels for 73%

profile of v2, /device:TPU:0, one launch (start us, length us, event | category | flops | bytes accessed | tf_op | source)
XLA Modules:
  0.0 582.5 jit_solution(5089115075544827294)
XLA Ops:
  7.8 1.3 multiply_reduce_fusion.2
  9.8 0.6 broadcast_in_dim.165.x_ref
  10.4 9.8 %table.1 = s32[8,8,128]{2,1,0:T(8,128)} custom-call(s32[8,128]{1,0:T(8,128)} %broadcast_in_dim.165.x_ref), custom_call_target="tpu_custom_call" | custom-call | tf_op jit(solution)/shard_map/table/pallas_call | solution.py:490
  20.2 1.0 slice_reduce_fusion.5
  21.1 0.8 select_reduce_fusion.1
  22.0 538.7 %conditional.1 = (bf16[1536,1280]{1,0:T(8,128)(2,1)S(1)}, f32[1536,1280]{1,0:T(8,128)S(1)}, f32[320,1280]{1,0:T(8,128)S(1)}, f32[1280,1280]{1,0:T(8,128)}, f32[1...) conditional(s32[]{:T(128)} %clamp.3, (s32[8]{0:T(128)S(1)}, ...), branch_computations={%region_2.11_spmd, %region_11.50_spmd} | conditional | flops 383993184256 | bytes 1522713856 | solution.py:1387
  22.1 0.6 dynamic_slice.38
  22.9 0.6 dynamic_slice.37
  23.5 1.4 pad_add_fusion.info_ref
  24.9 0.5 copy-done.2
  25.4 5.6 pieces.1
  31.0 1.3 copy-done.6
  32.4 0.6 broadcast_in_dim.149.gain_ref
  33.0 0.6 broadcast_in_dim.150.shift_ref
  33.7 1.0 copy.82.bias_t_ref
  34.7 3.4 copy.81.w_ref
  38.1 129.0 %pack_gather.1 = (bf16[96,1280]{1,0:T(8,128)(2,1)}, bf16[3072,1280]{1,0:T(8,128)(2,1)}, bf16[3072,640]{1,0:T(8,128)(2,1)}, bf16[960,3072]{1,0:T(8,128)(2,1)}) custom-call(bf16[8,96,1280]{2,1,0:T(8,128)(2,1)} %copy-done.6, bf16[1280,960]{1,0:T(8,128)(2,1)} %copy.81.w_ref, bf16[960,1280]{1,0:T(8,128)(2,1)S(1)} %bitcast.92, f32[1,960]{1,0:T(1,128)} %bitcast.114, ...), custom_call_target="tpu_custom_call" | custom-call | flops 89999998976 | bytes 270000000 | tf_op jit(solution)/shard_map/cond/branch_0_fun/pack_gather/pallas_call | solution.py:726
  167.2 2.7 copy-done.7
  169.9 2.1 copy-done.8
  172.0 7.0 %attend.1 = (bf16[384,320]{1,0:T(8,128)(2,1)S(1)}, bf16[384,128]{1,0:T(8,128)(2,1)S(1)}) custom-call(s32[8]{0:T(128)S(1)} %select_reduce_fusion.offset_ref, s32[8]{0:T(128)S(1)} %get-tuple-element.197.length_ref, bf16[960,3072]{1,0:T(8,128)(2,1)S(1)} %copy-done.7, bf16[3072,640]{1,0:T(8,128)(2,1)S(1)} %copy-done.8), custom_call_target="tpu_custom_call" | custom-call | flops 10000000000 | bytes 30000000 | tf_op jit(solution)/shard_map/cond/branch_0_fun/attend/pallas_call | solution.py:1135
  179.0 0.9 pad_maximum_fusion.3
  180.1 0.6 broadcast_in_dim.154.bias_ref
  180.7 0.7 convolution_convert_fusion.11
  181.4 75.3 %first_exchange.1 = (f32[96,1280]{1,0:T(8,128)S(1)}, bf16[3072,1280]{1,0:T(8,128)(2,1)S(1)}) custom-call(bf16[4,96,1280]{2,1,0:T(8,128)(2,1)S(1)} %bitcast.79, bf16[96,1280]{1,0:T(8,128)(2,1)S(1)} %copy-done.12, f32[1,1280]{1,0:T(1,128)S(1)} %broadcast_in_dim.151.bias_ref, f32[1,1280]{1,0:T(1,128)S(1)} %broadcast_in_dim.152.gain_ref, ...), custom_call_target="tpu_custom_call" | custom-call | flops 60000002048 | bytes 180000000 | tf_op jit(solution)/shard_map/cond/branch_0_fun/first_exchange/pallas_call | solution.py:870
  256.7 0.8 copy-done.11
  257.5 14.2 %multiply_convert_fusion.2 = (bf16[3072,1280]{1,0:T(8,128)(2,1)S(1)}, f32[3072,1280]{1,0:T(8,128)}) fusion(f32[1280]{0:T(1024)S(1)} %copy-done.74, bf16[3072,1280]{1,0:T(8,128)(2,1)S(1)} %get-tuple-element.226.act_ref, bf16[1280,1280]{1,0:T(8,128)(2,1)S(1)} %copy-done.71), kind=kOutput, calls=%fused_computation.104 | convolution fusion | flops 10089922560 | bytes 34739200 | tf_op jit(solution)/shard_map/cond/branch_0_fun/dot_general | solution.py:1312
  271.7 3.1 copy-done.76
  274.8 2.4 convolution_convert_fusion.12
  277.2 19.7 %fusion.74 = (f32[1280]{0:T(1024)}, bf16[3072,1280]{1,0:T(8,128)(2,1)S(1)}) fusion(f32[3072,1280]{1,0:T(8,128)} %get-tuple-element.408, f32[1280]{0:T(1024)S(1)} %copy-done.74, bf16[1280,1280]{1,0:T(8,128)(2,1)} %get-tuple-element.217, bf16[1,3072,1280]{2,1,0:T(8,128)(2,1)} %all-gather.9.cloned.1.call-done), kind=kOutput, calls=%fused_computation.146 | convolution fusion | flops 10113514496 | bytes 34744320 | tf_op jit(solution)/shard_map/cond/branch_0_fun/dot_general | solution.py:47
  296.9 3.0 convolution_convert_fusion.13
  300.3 88.5 %second_exchange.1 = (f32[96,1280]{1,0:T(8,128)}, bf16[96,1280]{1,0:T(8,128)(2,1)}, f32[8,1280]{1,0:T(8,128)}, bf16[3072,1280]{1,0:T(8,128)(2,1)}, f32[1280,1280...) custom-call(bf16[4,96,1280]{2,1,0:T(8,128)(2,1)} %bitcast.118, ...), custom_call_target="tpu_custom_call" | custom-call | flops 80000000000 | bytes 240000000 | tf_op jit(solution)/shard_map/cond/branch_0_fun/second_exchange/pallas_call | solution.py:942
  388.9 1.4 slice_convert_fusion.1
  390.4 0.5 copy.83
  390.9 4.3 fusion.75
  395.2 2.8 copy.84.ctxt_ref
  398.0 1.5 copy-done.10
  399.6 60.5 %attend_back.1.dt_ref = bf16[960,3072]{1,0:T(8,128)(2,1)} custom-call(s32[8]{0:T(128)S(1)} %copy-done.5, s32[8]{0:T(128)S(1)} %copy-done.65, bf16[3072,640]{1,0:T(8,128)(2,1)} %get-tuple-element.219.kv_ref, bf16[960,3072]{1,0:T(8,128)(2,1)} %get-tuple-element.218.qkvt_ref.qkt_ref, bf16[320,3072]{1,0:T(8,128)(2,1)S(1)} %copy-done.10, ...), custom_call_target="tpu_custom_call" | custom-call | flops 60000002048 | bytes 180000000 | tf_op jit(solution)/shard_map/cond/branch_0_fun/attend_back/pallas_call | solution.py:1217
  460.1 3.3 convolution_convert_fusion.10
  463.4 65.1 %third_exchange.1 = (bf16[3072,1280]{1,0:T(8,128)(2,1)}, f32[256,1280]{1,0:T(8,128)}, f32[3,1280,320]{2,1,0:T(8,128)}, f32[320,1280]{1,0:T(8,128)S(1)}) custom-call(bf16[4,96,1280]{2,1,0:T(8,128)(2,1)} %bitcast.110, bf16[96,1280]{1,0:T(8,128)(2,1)} %get-tuple-element.222.x_ref, f32[96,1280]{1,0:T(8,128)} %get-tuple-element.234.dmid_ref, ...), custom_call_target="tpu_custom_call" | custom-call | flops 60000002048 | bytes 180000000 | tf_op jit(solution)/shard_map/cond/branch_0_fun/third_exchange/pallas_call | solution.py:1018
  528.5 7.4 %copy.85 = f32[1280,3,320]{0,2,1:T(8,128)} copy(f32[1280,3,320]{2,0,1:T(8,128)} %bitcast.99) | data formatting | bytes 9830400 | tf_op jit(solution)/shard_map/cond
  536.0 1.5 slice_reduce_fusion
  537.5 3.3 convert_reduce_fusion.2
  540.8 4.9 convert_reduce_fusion.1
  545.7 3.2 copy-done
  549.0 3.5 unpack.1
  560.8 1.2 copy.138
  561.9 10.7 %copy.139 = f32[1280,1280]{1,0:T(8,128)} copy(f32[1280,1280]{1,0:T(8,128)} %get-tuple-element.483) | data formatting | bytes 13107200
  572.7 2.8 copy.140
  (96 shorter events, 1.3 us)
Async XLA Ops:
  22.0 145.2 %copy-start.64 = (s32[8]{0:T(128)}, s32[8]{0:T(128)S(1)}, u32[]{:S(2)}) copy-start(s32[8]{0:T(128)S(1)} %get-tuple-element.197.length_ref) | copy-start | bytes 100 | tf_op jit(solution)/shard_map/cond
  22.0 10.3 %copy-start.49 = (f32[1280]{0:T(1024)S(1)}, f32[1280]{0:T(1024)}, u32[]{:S(2)}) copy-start(f32[1280]{0:T(1024)} %get-tuple-element.213) | copy-start | bytes 15364 | tf_op jit(solution)/shard_map/cond
  22.0 10.9 %copy-start.59 = (f32[1280]{0:T(1024)S(1)}, f32[1280]{0:T(1024)}, u32[]{:S(2)}) copy-start(f32[1280]{0:T(1024)} %get-tuple-element.214) | copy-start | bytes 15364 | tf_op jit(solution)/shard_map/cond
  22.1 11.5 %copy-start.55 = (f32[320]{0:T(512)S(1)}, f32[320]{0:T(512)}, u32[]{:S(2)}) copy-start(f32[320]{0:T(512)} %get-tuple-element.211) | copy-start | bytes 3844 | tf_op jit(solution)/shard_map/cond
  22.1 11.5 %copy-start.57 = (f32[320]{0:T(512)S(1)}, f32[320]{0:T(512)}, u32[]{:S(2)}) copy-start(f32[320]{0:T(512)} %get-tuple-element.212) | copy-start | bytes 3844 | tf_op jit(solution)/shard_map/cond
  22.1 12.6 %copy-start.25 = (bf16[1280,3,320]{0,2,1:T(8,128)(2,1)S(1)}, bf16[1280,3,320]{0,2,1:T(8,128)(2,1)}, u32[]{:S(2)}) copy-start(bf16[1280,3,320]{0,2,1:T(8,128)(2,1)} %get-tuple-element.210) | copy-start | bytes 7372804 | tf_op jit(solution)/shard_map/cond
  22.1 145.0 %reduce-scatter.2.cloned.1.call-start = ((), (), s32[]{:S(2)}) async-start(), calls=%async_computation.1 | async-start | bytes 2211840 | tf_op jit(solution)/shard_map/cond/branch_0_fun/reduce_scatter | solution.py:1297
  22.9 144.3 %copy-start.4 = (s32[8]{0:T(128)}, s32[8]{0:T(128)S(1)}, u32[]{:S(2)}) copy-start(s32[8]{0:T(128)S(1)} %select_reduce_fusion.offset_ref) | copy-start | bytes 100 | tf_op jit(solution)/shard_map/cond
  24.9 0.5 copy-start.2
  31.0 1.3 copy-start.6
  32.3 244.9 %all-gather.9.cloned.1.call-start = ((), (), s32[]{:S(2)}) async-start(), calls=%async_computation.4 | async-start | bytes 8110080 | tf_op jit(solution)/shard_map/cond/branch_0_fun/all_gather | solution.py:1299
  33.7 4.4 copy-start.54
  167.1 221.8 %all-gather.7.cloned.1.call-start = ((), (), s32[]{:S(2)}) async-start(), calls=%async_computation.3 | async-start | bytes 3538944 | tf_op jit(solution)/shard_map/cond/branch_0_fun/all_gather | solution.py:1306
  167.2 2.7 copy-start.7
  169.9 2.1 copy-start.8
  172.0 8.0 %copy-start.45 = (f32[1280]{0:T(1024)S(1)}, f32[1280]{0:T(1024)}, u32[]{:S(2)}) copy-start(f32[1280]{0:T(1024)} %get-tuple-element.224) | copy-start | bytes 15364 | tf_op jit(solution)/shard_map/cond
  172.0 8.0 %copy-start.41 = (f32[1280]{0:T(1024)S(1)}, f32[1280]{0:T(1024)}, u32[]{:S(2)}) copy-start(f32[1280]{0:T(1024)} %get-tuple-element.223) | copy-start | bytes 15364 | tf_op jit(solution)/shard_map/cond
  172.0 8.1 %copy-start.62 = (f32[1280]{0:T(1024)S(1)}, f32[1280]{0:T(1024)}, u32[]{:S(2)}) copy-start(f32[1280]{0:T(1024)} %get-tuple-element.225) | copy-start | bytes 15364 | tf_op jit(solution)/shard_map/cond
  172.0 8.1 %copy-start.52 = (f32[1280]{0:T(1024)S(1)}, f32[1280]{0:T(1024)}, u32[]{:S(2)}) copy-start(f32[1280]{0:T(1024)} %get-tuple-element.230) | copy-start | bytes 15364 | tf_op jit(solution)/shard_map/cond
  172.0 8.7 %copy-start.31 = (bf16[320,1280]{1,0:T(8,128)(2,1)S(1)}, bf16[320,1280]{1,0:T(8,128)(2,1)}, u32[]{:S(2)}) copy-start(bf16[320,1280]{1,0:T(8,128)(2,1)} %get-tuple-element.221.wout_ref) | copy-start | bytes 2457604 | tf_op jit(solution)/shard_map/cond
  172.0 9.3 %copy-start.12 = (bf16[96,1280]{1,0:T(8,128)(2,1)S(1)}, bf16[96,1280]{1,0:T(8,128)(2,1)}, u32[]{:S(2)}) copy-start(bf16[96,1280]{1,0:T(8,128)(2,1)} %get-tuple-element.222.x_ref) | copy-start | bytes 737284 | tf_op jit(solution)/shard_map/cond
  179.9 365.8 %all-gather.5.cloned.1.call-start = ((), (), s32[]{:S(2)}) async-start(), calls=%async_computation.2 | async-start | bytes 8110080 | tf_op jit(solution)/shard_map/cond/branch_0_fun/all_gather | solution.py:1325
  180.0 76.7 %copy-start.1 = (f32[1,1280]{1,0:T(1,128)}, f32[1,1280]{1,0:T(1,128)S(1)}, u32[]{:S(2)}) copy-start(f32[1,1280]{1,0:T(1,128)S(1)} %broadcast_in_dim.152.gain_ref) | copy-start | bytes 15364 | tf_op jit(solution)/shard_map/cond
  181.4 76.1 %copy-start.71 = (bf16[1280,1280]{1,0:T(8,128)(2,1)S(1)}, bf16[1280,1280]{1,0:T(8,128)(2,1)}, u32[]{:S(2)}) copy-start(bf16[1280,1280]{1,0:T(8,128)(2,1)} %get-tuple-element.227) | copy-start | bytes 9830404 | tf_op jit(solution)/shard_map/cond
  181.4 76.1 %copy-start.74 = (f32[1280]{0:T(1024)S(1)}, f32[1280]{0:T(1024)}, u32[]{:S(2)}) copy-start(f32[1280]{0:T(1024)} %get-tuple-element.228) | copy-start | bytes 15364 | tf_op jit(solution)/shard_map/cond
  256.7 0.8 copy-start.11
  257.5 14.2 %copy-start.9 = (bf16[3072,1280]{1,0:T(8,128)(2,1)}, bf16[3072,1280]{1,0:T(8,128)(2,1)S(1)}, u32[]{:S(2)}) copy-start(bf16[3072,1280]{1,0:T(8,128)(2,1)S(1)} %get-tuple-element.226.act_ref) | copy-start | bytes 23592964 | tf_op jit(solution)/shard_map/cond
  257.5 17.3 %copy-start.69 = (bf16[1280,1280]{1,0:T(8,128)(2,1)S(1)}, bf16[1280,1280]{1,0:T(8,128)(2,1)}, u32[]{:S(2)}) copy-start(bf16[1280,1280]{1,0:T(8,128)(2,1)} %get-tuple-element.217) | copy-start | bytes 9830404 | tf_op jit(solution)/shard_map/cond
  271.7 3.1 copy-start.76
  277.2 19.7 %copy-start.72 = (bf16[1280,1280]{1,0:T(8,128)(2,1)S(1)}, bf16[1280,1280]{1,0:T(8,128)(2,1)}, u32[]{:S(2)}) copy-start(bf16[1280,1280]{1,0:T(8,128)(2,1)} %get-tuple-element.227) | copy-start | bytes 9830404 | tf_op jit(solution)/shard_map/cond
  296.9 3.4 copy-start.77
  388.9 9.1 %copy-start.5 = (s32[8]{0:T(128)S(1)}, s32[8]{0:T(128)}, u32[]{:S(2)}) copy-start(s32[8]{0:T(128)} %copy-done.4) | copy-start | bytes 100 | tf_op jit(solution)/shard_map/cond
  388.9 9.1 %copy-start.65 = (s32[8]{0:T(128)S(1)}, s32[8]{0:T(128)}, u32[]{:S(2)}) copy-start(s32[8]{0:T(128)} %copy-done.64) | copy-start | bytes 100 | tf_op jit(solution)/shard_map/cond
  398.0 1.5 copy-start.10
  399.6 60.5 %copy-start.26 = (bf16[1280,3,320]{0,2,1:T(8,128)(2,1)S(1)}, bf16[1280,3,320]{0,2,1:T(8,128)(2,1)}, u32[]{:S(2)}) copy-start(bf16[1280,3,320]{0,2,1:T(8,128)(2,1)} %get-tuple-element.210) | copy-start | bytes 7372804 | tf_op jit(solution)/shard_map/cond
  528.5 7.4 %copy-start.38 = (f32[256,1280]{1,0:T(8,128)S(1)}, f32[256,1280]{1,0:T(8,128)}, u32[]{:S(2)}) copy-start(f32[256,1280]{1,0:T(8,128)} %get-tuple-element.246) | copy-start | bytes 3932164 | tf_op jit(solution)/shard_map/cond
  535.9 9.8 %copy-start.3 = (s32[2]{0:T(128)S(1)}, s32[2]{0:T(128)}, u32[]{:S(2)}) copy-start(s32[2]{0:T(128)} %copy-done.2) | copy-start | bytes 28 | tf_op jit(solution)/shard_map/cond
  545.7 3.2 copy-start
  560.7 11.9 %copy-start.66 = (f32[1536,1280]{1,0:T(8,128)}, f32[1536,1280]{1,0:T(8,128)S(1)}, u32[]{:S(2)}) copy-start(f32[1536,1280]{1,0:T(8,128)S(1)} %get-tuple-element.477) | copy-start | bytes 23592964
  560.8 11.9 %copy-start.68 = (bf16[1536,1280]{1,0:T(8,128)(2,1)}, bf16[1536,1280]{1,0:T(8,128)(2,1)S(1)}, u32[]{:S(2)}) copy-start(bf16[1536,1280]{1,0:T(8,128)(2,1)S(1)} %get-tuple-element.476) | copy-start | bytes 11796484
  560.8 11.9 %slice-start.2 = ((s8[6553600]{0:T(1024)(128)(4,1)}), s8[4194304]{0:T(1024)(128)(4,1)S(1)}, s32[]{:S(2)}) async-start(s8[6553600]{0:T(1024)(128)(4,1)} %bitcast.97), calls=%async_computation.11 | async-start | bytes 8388608
  561.9 10.7 %slice-start.3 = ((s8[6553600]{0:T(1024)(128)(4,1)}), s8[2359296]{0:T(1024)(128)(4,1)S(1)}, s32[]{:S(2)}) async-start(s8[6553600]{0:T(1024)(128)(4,1)} %bitcast.97), calls=%async_computation.12 | async-start | bytes 4718592
Sparse Core Ops, SparseCore 0:
  32.4 76.8 reduce-scatter.1
  167.2 91.4 all-gather.8
  261.7 64.5 all-gather.6
  389.0 72.4 all-gather.4
